TPU v7x, 256 devices: a whole 4x4x8 slice. The times are simulated.
256 devices in a mesh: exp: 32 (over y, z_lo, core), feat: 8 (over z_hi, x).
Axes of the slice: x: 4, y: 4, z: 8 (z_hi: 2, z_lo: 4; z = z_hi * 4 + z_lo), core: 2. Of those that a mesh axis runs over, the one named last changes fastest.
Arguments:
- tokens: bfloat16 [512, 7168], P('exp', 'feat'), may hold values from -6 to 6
- route_ids: int32 [512, 8], P('exp'), may hold values from 0 to 31, all different within a row
- route_weights: float32 [512, 8], P('exp'), may hold values from 0.05 to 0.6
- gate_proj: bfloat16 [32, 7168, 1024], P('exp', 'feat'), may hold values from -0.0625 to 0.0625
- up_proj: bfloat16 [32, 7168, 1024], P('exp', 'feat'), may hold values from -0.0625 to 0.0625
- down_proj: bfloat16 [32, 1024, 7168], P('exp', None, 'feat'), may hold values from -0.1875 to 0.1875
- enc_weight: bfloat16 [7168, 65536], P('feat', 'exp'), may hold values from -0.0625 to 0.0625
- enc_bias: float32 [65536], P('exp'), may hold values from -3 to 3
- dec_weight: bfloat16 [65536, 7168], P('exp', 'feat'), may hold values from -0.0234375 to 0.0234375
- dec_bias: float32 [7168], P('feat'), may hold values from -3 to 3
- clamp_ids: int32 [64], replicated, may hold values from 0 to 65535, as said below
- clamp_values: bfloat16 [64], replicated, may hold values from 8 to 30
Outputs:
- error_term: float32 [512, 7168], P('exp', 'feat')
- steered: float32 [512, 7168], P('exp', 'feat')
Inputs may be any that keep to these rules, and one draw needn't show every extreme that they name: `route_ids`: each token names 8 different experts. `clamp_ids`: 64 different features.
All inputs are finite; a program needn't handle non-finite values.
Results may differ from a plain program's by a relative error of at most 0.0035.
Values may be sent and summed in bfloat16 or wider, within the bound.
A program may use at most 64 MiB of HBM per device.

v0:
```python
import jax
import jax.numpy as jnp
from jax import lax
from jax.sharding import PartitionSpec as P

SLOT = 8


def local_codes(route_ids, slot_limit, expert_count):
    flat_ids = route_ids.reshape(-1)
    experts = jnp.arange(expert_count, dtype=jnp.int32)
    onehot = (flat_ids[:, None] == experts[None, :]).astype(jnp.int32)
    before = jnp.sum(jnp.cumsum(onehot, axis=0) * onehot, axis=1) - 1
    slot_code = jnp.where(before < slot_limit, flat_ids * slot_limit + before, -1)
    return slot_code.reshape(route_ids.shape)


def local(
    tokens,
    route_ids,
    route_weights,
    gate_proj,
    up_proj,
    down_proj,
    enc_weight,
    enc_bias,
    dec_weight,
    dec_bias,
    clamp_ids,
    clamp_values,
):
    expert_count = lax.axis_size("exp")
    row_count, shard_width = tokens.shape
    capacity = expert_count * SLOT
    slot_code = local_codes(route_ids, SLOT, expert_count)
    targets = jnp.arange(capacity, dtype=jnp.int32)
    matches = slot_code[None, :, :] == targets[:, None, None]
    partial_pre = jnp.dot(
        lax.all_gather(tokens, "exp", axis=0, tiled=True),
        enc_weight,
        preferred_element_type=jnp.float32,
    )
    picker = jnp.any(matches, axis=2).astype(jnp.bfloat16)
    outgoing = jnp.dot(picker, tokens, preferred_element_type=jnp.float32).astype(jnp.bfloat16)
    incoming = lax.all_to_all(
        outgoing.reshape(expert_count, SLOT, shard_width),
        "exp",
        split_axis=0,
        concat_axis=0,
        tiled=True,
    )
    expert_in = incoming.reshape(capacity, shard_width)
    gate_part = jnp.dot(expert_in, gate_proj[0], preferred_element_type=jnp.float32)
    up_part = jnp.dot(expert_in, up_proj[0], preferred_element_type=jnp.float32)
    pre_sum, gate_sum, up_sum = lax.psum((partial_pre, gate_part, up_part), "feat")
    feature_act = jax.nn.relu(pre_sum + enc_bias).astype(jnp.bfloat16)
    hidden = (jax.nn.silu(gate_sum) * up_sum).astype(jnp.bfloat16)
    expert_out = jnp.dot(hidden, down_proj[0], preferred_element_type=jnp.float32).astype(
        jnp.bfloat16
    )
    returned = lax.all_to_all(
        expert_out.reshape(expert_count, SLOT, shard_width),
        "exp",
        split_axis=0,
        concat_axis=0,
        tiled=True,
    )
    weighted = jnp.sum(jnp.where(matches, route_weights[None, :, :], 0.0), axis=2)
    returned_rows = returned.reshape(capacity, shard_width).astype(jnp.float32)
    moe_out = jnp.einsum("cr,cd->rd", weighted, returned_rows, precision=lax.Precision.HIGHEST)
    feature_count = enc_weight.shape[1]
    feature_base = lax.axis_index("exp") * feature_count
    local_ids = clamp_ids - feature_base
    inside = (local_ids >= 0) & (local_ids < feature_count)
    safe_ids = jnp.clip(local_ids, 0, feature_count - 1)
    chosen = jnp.take(feature_act, safe_ids, axis=1).astype(jnp.float32)
    change = jnp.where(inside[None, :], clamp_values.astype(jnp.float32)[None, :] - chosen, 0.0)
    rows_dec = jnp.take(dec_weight, safe_ids, axis=0).astype(jnp.float32)
    shift_part = jnp.dot(change, rows_dec, precision=lax.Precision.HIGHEST)
    rebuilt_rows = jnp.dot(feature_act, dec_weight, preferred_element_type=jnp.float32)
    summed = lax.psum_scatter(
        jnp.concatenate([rebuilt_rows, shift_part], axis=1), "exp", scatter_dimension=0, tiled=True
    )
    rebuilt = summed[:, :shard_width]
    clamp_shift = summed[:, shard_width:]
    error_term = moe_out - rebuilt - dec_bias
    steered = moe_out + clamp_shift
    return (error_term, steered)


def solution(mesh):
    placed = (
        P("exp", "feat"),
        P("exp", None),
        P("exp", None),
        P("exp", "feat", None),
        P("exp", "feat", None),
        P("exp", None, "feat"),
        P("feat", "exp"),
        P("exp"),
        P("exp", "feat"),
        P("feat"),
        P(),
        P(),
    )
    return jax.shard_map(
        local,
        mesh=mesh,
        in_specs=placed,
        out_specs=(P("exp", "feat"), P("exp", "feat")),
        check_vma=False,
    )
```

profile of v0, /device:TPU:1, one launch (start us, length us, event | category | flops | bytes accessed | tf_op | source)
XLA Modules:
  0.0 522.2 jit_solution(13151066521996460914)
XLA Ops:
  7.2 0.0 copy-start
  7.2 0.9 copy.22
  8.1 0.1 eq.28
  8.2 0.1 fusion.28
  8.3 0.2 reduce_window_sum.11
  8.4 0.2 select_reduce_fusion.1
  8.6 0.1 sub.32
  8.7 0.1 fusion.22
  8.8 1.8 fusion.9
  10.7 10.2 %all-to-all-start = ((bf16[32,8,896]{2,1,0:T(8,128)(2,1)}), bf16[32,8,896]{2,1,0:T(8,128)(2,1)S(1)}, u32[]{:S(2)}, u32[]{:S(2)}) async-start(bf16[32,8,896]{2,1,0:T(8,128)(2,1)} %fusion.9), calls=%async_computation | async-start | bytes 917504 | tf_op jit(solution)/shard_map/all_to_all | solution.py:45
  20.9 0.0 all-reduce.3.cloned.1.call-start
  20.9 48.5 %all_gather.3 = bf16[512,896]{1,0:T(8,128)(2,1)S(1)} all-gather(bf16[16,896]{1,0:T(8,128)(2,1)} %param.12), channel_id=1, replica_groups=mesh['exp'=32,'feat'=8] {'exp'}, dimensions={0}, use_global_device_ids=true | all-gather | bytes 946176 | tf_op jit(solution)/shard_map/all_gather | solution.py:39
  69.4 6.4 %fusion.37 = f32[512,2048]{1,0:T(8,128)} fusion(bf16[512,896]{1,0:T(8,128)(2,1)S(1)} %all_gather.3, bf16[896,2048]{1,0:T(8,128)(2,1)} %param.18), kind=kOutput, calls=%fused_computation.51 | convolution fusion | flops 1879048192 | bytes 8781824 | tf_op jit(solution)/shard_map/dot_general | solution.py:38
  75.8 0.0 all-to-all-done
  75.8 0.0 copy-done
  75.8 0.0 copy-start.2
  75.8 1.7 fusion.2
  77.5 0.0 copy-done.2
  77.5 1.7 fusion.4
  79.2 0.0 copy-start.6
  79.2 0.0 copy-start.3
  79.2 0.0 all-reduce.3.cloned.1.call-update
  79.2 0.0 reduce-scatter.2.cloned.1.call-start
  79.3 0.6 copy-done.8
  79.9 0.0 copy-done.6
  79.9 3.3 gather_fusion.1
  83.2 267.2 %all-reduce.3.cloned.1.call-done = (f32[256,1024]{1,0:T(8,128)}, f32[256,1024]{1,0:T(8,128)}, f32[512,2048]{1,0:T(8,128)}) async-done(((f32[256,1024]{1,0:T(8,128)}, f32[256,1024]{1,0:T(8,128)}, f32[512,2048]{1,0:T(8,128)}), (f32[256,1024]{1,0:T(8,128)}, f32[256,1024]{1,0:T(8,128)}, f32[512,2048]{1,0:T(8,128)})) %all-reduce.3.cloned.1.call-update) | async-done | bytes 6291472 | tf_op jit(solution)/shard_map/psum | solution.py:55
  350.4 0.0 copy-done.3
  350.4 4.0 maximum_convert_fusion
  354.5 3.9 copy.25
  358.4 6.2 %fusion.38 = f32[512,896]{1,0:T(8,128)} fusion(bf16[512,2048]{1,0:T(8,128)(2,1)} %maximum_convert_fusion, bf16[2048,896]{1,0:T(8,128)(2,1)} %param.20), kind=kOutput, calls=%fused_computation.52 | convolution fusion | flops 1879048192 | bytes 7602176 | tf_op jit(solution)/shard_map/dot_general | solution.py:80
  364.6 2.6 gather_fusion
  367.2 0.0 copy-start.1
  367.2 1.0 fusion.18
  368.2 0.5 copy-done.1
  368.7 2.1 pad_maximum_fusion
  370.7 0.0 copy-start.7
  370.7 0.0 reduce-scatter.2.cloned.1.call-update
  370.7 1.2 copy-done.7
  371.9 3.4 fusion.10
  375.3 5.1 all-to-all-start.1
  380.5 0.0 copy-done.5
  380.5 0.1 copy.24
  380.6 0.1 select_reduce_fusion
  380.7 18.7 %all-to-all-done.1 = bf16[32,8,896]{2,1,0:T(8,128)(2,1)S(1)} async-done(((bf16[32,8,896]{2,1,0:T(8,128)(2,1)}), bf16[32,8,896]{2,1,0:T(8,128)(2,1)S(1)}, u32[]{:S(2)}, u32[]{:S(2)}) %all-to-all-start.1) | async-done | bytes 458784 | tf_op jit(solution)/shard_map/all_to_all | solution.py:61
  399.4 114.1 %reduce-scatter.2.cloned.1.call-done = f32[16,1792]{1,0:T(8,128)} async-done(((f32[512,1792]{1,0:T(8,128)}), f32[16,1792]{1,0:T(8,128)}) %reduce-scatter.2.cloned.1.call-update) | async-done | bytes 114704 | tf_op jit(solution)/shard_map/reduce_scatter | solution.py:81
  513.6 0.0 copy-done.4
  513.6 1.8 slice_add_fusion
  (8 shorter events, 0.0 us)
Async XLA Ops:
  7.2 68.6 %copy-start = (bf16[1,896,1024]{2,1,0:T(8,128)(2,1)S(1)}, bf16[1,896,1024]{2,1,0:T(8,128)(2,1)}, u32[]{:S(2)}) copy-start(bf16[1,896,1024]{2,1,0:T(8,128)(2,1)} %param.16) | copy-start | bytes 5505028
  10.7 65.1 %all-to-all-start = ((bf16[32,8,896]{2,1,0:T(8,128)(2,1)}), bf16[32,8,896]{2,1,0:T(8,128)(2,1)S(1)}, u32[]{:S(2)}, u32[]{:S(2)}) async-start(bf16[32,8,896]{2,1,0:T(8,128)(2,1)} %fusion.9), calls=%async_computation | async-start | bytes 917504 | tf_op jit(solution)/shard_map/all_to_all | solution.py:45
  20.9 329.5 %all-reduce.3.cloned.1.call-start = ((), (), s32[]{:S(2)}) async-start(), calls=%async_computation.4 | async-start | bytes 12582912 | tf_op jit(solution)/shard_map/psum | solution.py:55
  75.8 1.7 copy-start.2
  79.2 0.7 copy-start.8
  79.2 0.7 copy-start.6
  79.2 271.2 %copy-start.3 = (f32[2048]{0:T(1024)S(1)}, f32[2048]{0:T(1024)}, u32[]{:S(2)}) copy-start(f32[2048]{0:T(1024)} %param.19) | copy-start | bytes 24580
  79.2 434.3 %reduce-scatter.2.cloned.1.call-start = ((), (), s32[]{:S(2)}) async-start(), calls=%async_computation.3 | async-start | bytes 3784704 | tf_op jit(solution)/shard_map/reduce_scatter | solution.py:81
  367.2 1.5 copy-start.1
  370.7 1.2 copy-start.7
  371.9 8.5 %copy-start.5 = (f32[16,8]{0,1:T(8,128)S(1)}, f32[16,8]{0,1:T(8,128)}, u32[]{:S(2)}) copy-start(f32[16,8]{0,1:T(8,128)} %param.14) | copy-start | bytes 1540
  371.9 141.6 %copy-start.4 = (f32[896]{0:T(1024)S(1)}, f32[896]{0:T(1024)}, u32[]{:S(2)}) copy-start(f32[896]{0:T(1024)} %param.21) | copy-start | bytes 10756
  375.3 24.1 %all-to-all-start.1 = ((bf16[32,8,896]{2,1,0:T(8,128)(2,1)}), bf16[32,8,896]{2,1,0:T(8,128)(2,1)S(1)}, u32[]{:S(2)}, u32[]{:S(2)}) async-start(bf16[32,8,896]{2,1,0:T(8,128)(2,1)} %fusion.10), calls=%async_computation.1 | async-start | bytes 917504 | tf_op jit(solution)/shard_map/all_to_all | solution.py:61
Sparse Core Ops, SparseCore 0:
  79.3 271.0 all-reduce.2
  370.9 142.6 reduce-scatter.1
where the time goes:
time: 526 us; the launch traced here: 522 us
  waiting for transfers between devices  400 us (76%)
  blocking collectives  48.5 us (9%)
  matrix products  24 us (5%)
  starting transfers between devices  15.4 us (3%)
  between operations  14.2 us (3%)
  local copies, waits for them, and re-layouts  13.2 us (3%)
  other arithmetic  6.81 us (1%)
    psum x1, waiting for transfers between devices, local(): lax.psum((partial_pre, gate_part, up_part), 'feat')  267 us
    reduce_scatter x1, waiting for transfers between devices, local(): lax.psum_scatter(jnp.concatenate([rebuilt_rows, shift_part], axis=1), 'ex...  114 us
    all_gather x1, blocking collectives, local(): lax.all_gather(tokens, 'exp', axis=0, tiled=True)  48.5 us
    all_to_all x1, waiting for transfers between devices, local(): lax.all_to_all(expert_out.reshape(expert_count, SLOT, shard_width), 'exp'...  18.7 us
  transfers between devices with their start and end apart: 4, of which 3 were waited for; matrix products, arithmetic and copies ran while one was open for 3% of the time, Pallas kernels for 0%

commit v1 on v0

v1 whole, which is shorter than its diff:
```python
import functools

import jax
import jax.numpy as jnp
from jax import lax
from jax.experimental import pallas as pl
from jax.experimental.pallas import tpu as pltpu
from jax.sharding import PartitionSpec as P

SLOT = 8
ROWS = 16
WIDTH = 896
EXTRA = 128
WIDE = WIDTH + EXTRA
FEATURES = 2048
HIDDEN = 1024
CHIPS = 16
EXPERTS = 32
CHUNKS = 4
CHUNK_ROWS = 128
MESH = pl.DeviceIdType.MESH
F32 = jnp.float32
BF16 = jnp.bfloat16


def remote(src, dst, send_sem, recv_sem, device):
    return pltpu.make_async_remote_copy(
        src_ref=src,
        dst_ref=dst,
        send_sem=send_sem,
        recv_sem=recv_sem,
        device_id=device,
        device_id_type=MESH,
    )


def dot(a, b):
    return jnp.dot(a, b, preferred_element_type=F32)


def kernel(
    tok_ref,
    route_ref,
    weight_ref,
    bias_ref,
    dbias_ref,
    ids_ref,
    values_ref,
    gate_hbm,
    up_hbm,
    down_hbm,
    enc_hbm,
    dec_hbm,
    err_ref,
    steered_ref,
    gate_w,
    up_w,
    down_w,
    enc_w,
    dec_w,
    tok_all,
    gu_own,
    gu_in,
    gu_zsend,
    gu_zin,
    pre_f32,
    pre_send,
    pre_in,
    z_send,
    z_in,
    z_own,
    act,
    hid,
    out_send,
    out_in,
    rec,
    mate_in,
    fin_send,
    fin_in,
    fin_own,
    combine,
    moe_ref,
    row_own,
    row_mate,
    row_part,
    row_in,
    row_sum,
    row_zin,
    rows_dec,
    load_sem,
    tok_s,
    tok_r,
    mate_s,
    mate_r,
    gux_s,
    gux_r,
    guz_s,
    guz_r,
    hz_s,
    hz_r,
    hx_s,
    hx_r,
    px_s,
    px_r,
    pz_s,
    pz_r,
    az_s,
    az_r,
    ax_s,
    ax_r,
    out_s,
    out_r,
    cm_s,
    cm_r,
    fin_s,
    fin_r,
    rm_s,
    rm_r,
    ry_s,
    ry_r,
    rz_s,
    rz_r,
    rg_s,
    rg_r,
):
    e = lax.axis_index("exp")
    f = lax.axis_index("feat")
    chip, core = e // 2, e % 2
    y, zl = chip // 4, chip % 4
    zh, x = f // 4, f % 4
    mate = {"exp": chip * 2 + (1 - core), "feat": f}
    zpeer = {"exp": e, "feat": (1 - zh) * 4 + x}

    def xpeer(k):
        return {"exp": e, "feat": zh * 4 + (x + k) % 4}

    loads = [
        pltpu.make_async_copy(gate_hbm.at[0], gate_w, load_sem.at[0]),
        pltpu.make_async_copy(up_hbm.at[0], up_w, load_sem.at[1]),
        pltpu.make_async_copy(enc_hbm, enc_w, load_sem.at[2]),
        pltpu.make_async_copy(down_hbm.at[0], down_w, load_sem.at[3]),
        pltpu.make_async_copy(dec_hbm, dec_w.at[:, pl.ds(0, WIDTH)], load_sem.at[4]),
    ]
    for load in loads:
        load.start()

    barrier = pltpu.get_barrier_semaphore()

    def greet(k, carry):
        pl.semaphore_signal(
            barrier, inc=1, device_id={"exp": (e + k) % EXPERTS, "feat": f}, device_id_type=MESH
        )
        return carry

    lax.fori_loop(1, EXPERTS, greet, 0)
    for k in range(1, 4):
        pl.semaphore_signal(barrier, inc=1, device_id=xpeer(k), device_id_type=MESH)
    pl.semaphore_signal(barrier, inc=1, device_id=zpeer, device_id_type=MESH)
    lane = lax.broadcasted_iota(jnp.int32, (ROWS, EXTRA), 1)
    named = jnp.zeros((ROWS, EXTRA), F32)
    spread = jnp.zeros((ROWS, EXTRA), F32)
    for k in range(route_ref.shape[1]):
        hit = route_ref[:, k : k + 1] == lane
        named = jnp.where(hit, 1.0, named)
        spread = jnp.where(hit, weight_ref[:, k : k + 1], spread)
    earlier = jnp.where(
        lax.broadcasted_iota(jnp.int32, (ROWS, ROWS), 0)
        > lax.broadcasted_iota(jnp.int32, (ROWS, ROWS), 1),
        1.0,
        0.0,
    ).astype(BF16)
    before = dot(earlier, named.astype(BF16))
    code = jnp.where((named > 0) & (before < SLOT), before + 1.0, 0.0).astype(BF16)
    tok_all[e, :, pl.ds(0, WIDTH)] = tok_ref[...]
    tok_all[e, :, pl.ds(WIDTH, EXTRA)] = code
    pl.semaphore_wait(barrier, EXPERTS - 1 + 4)

    def token_copy(k):
        there = (chip + k) % CHIPS
        return remote(
            tok_all.at[e],
            tok_all.at[e],
            tok_s.at[k],
            tok_r.at[k],
            {"exp": there * 2 + core, "feat": f},
        )

    def token_pass(k):
        block = ((chip + CHIPS - k) % CHIPS) * 2 + core
        return remote(tok_all.at[block], tok_all.at[block], mate_s.at[k], mate_r.at[k], mate)

    def token_start(k, carry):
        token_copy(k).start()
        return carry

    lax.fori_loop(1, CHIPS, token_start, 0)
    token_pass(0).start()

    def token_forward(k, carry):
        token_copy(k).wait_recv()
        token_pass(k).start()
        return carry

    lax.fori_loop(1, CHIPS, token_forward, 0)

    slot_lane = lax.broadcasted_iota(jnp.int32, (EXTRA, EXPERTS * SLOT), 1)
    widen = jnp.where(
        (slot_lane >> 3) == lax.broadcasted_iota(jnp.int32, (EXTRA, EXPERTS * SLOT), 0), 1.0, 0.0
    ).astype(BF16)
    slot_wanted = (
        (lax.broadcasted_iota(jnp.int32, (ROWS, EXPERTS * SLOT), 1) & 7) + 1
    ).astype(F32)
    in_slot = dot(code, widen) == slot_wanted

    def three(value):
        high = value.astype(BF16)
        rest = value - high.astype(F32)
        middle = rest.astype(BF16)
        return high, middle, (rest - middle.astype(F32)).astype(BF16)

    for part, piece in enumerate(three(spread)):
        combine[part] = jnp.where(in_slot, dot(piece, widen), 0.0).astype(BF16)
    feature = lax.broadcasted_iota(jnp.int32, (FEATURES, EXTRA), 0) + e * FEATURES
    dec_w[:, pl.ds(WIDTH, EXTRA)] = jnp.where(feature == ids_ref[0:1, :], 1.0, 0.0).astype(BF16)

    def token_arrived(k, carry):
        token_pass(k).wait_recv()
        return carry

    lax.fori_loop(0, CHIPS, token_arrived, 0)

    everything = tok_all[...].reshape(EXPERTS * ROWS, WIDE)
    pick = jnp.where(lax.broadcasted_iota(jnp.int32, (8, EXTRA), 1) == e, 1.0, 0.0).astype(BF16)
    codes = lax.dot_general(
        pick, everything[:, WIDTH:], (((1,), (1,)), ((), ())), preferred_element_type=F32
    )
    slot_row = lax.broadcasted_iota(jnp.int32, (EXPERTS * SLOT, EXPERTS * ROWS), 0)
    token_col = lax.broadcasted_iota(jnp.int32, (EXPERTS * SLOT, EXPERTS * ROWS), 1)
    same_block = (slot_row >> 3) == (token_col >> 4)
    wanted = ((slot_row & 7) + 1).astype(F32)
    picker = jnp.where(same_block & (codes[0:1, :] == wanted), 1.0, 0.0).astype(BF16)
    expert_in = dot(picker, everything[:, :WIDTH]).astype(BF16)

    loads[0].wait()
    loads[1].wait()

    for half, weights in ((0, gate_w), (1, up_w)):

        def gate_tile(n, carry, half=half, weights=weights):
            at = pl.multiple_of(n * 256, 256)
            gu_own[:, pl.ds(pl.multiple_of(half * HIDDEN + n * 256, 256), 256)] = dot(
                expert_in, weights[:, pl.ds(at, 256)]
            )
            return carry

        lax.fori_loop(0, HIDDEN // 256, gate_tile, 0)

    def gux_copy(k):
        rows = pl.ds(((x + k) % 4) * 64, 64)
        return remote(gu_own.at[rows], gu_in.at[k - 1], gux_s.at[k - 1], gux_r.at[k - 1], xpeer(k))

    for k in (2, 1, 3):
        gux_copy(k).start()
    loads[2].wait()

    def blocks_of(j):
        return ((y + 1 + j) % 4) * 8

    def px_copy(j, k):
        rows = pl.ds(((x + k) % 4) * 32, 32)
        return remote(
            pre_send.at[j, rows], pre_in.at[j, k - 1], px_s.at[j, k - 1], px_r.at[j, k - 1], xpeer(k)
        )

    def pre_multiply(j):
        rows = tok_all[pl.ds(blocks_of(j), 8)].reshape(CHUNK_ROWS, WIDE)[:, :WIDTH]

        def tile(n, carry):
            at = pl.multiple_of(n * 256, 256)
            part = dot(rows, enc_w[:, pl.ds(at, 256)])
            pre_f32[j, :, pl.ds(at, 256)] = part
            pre_send[j, :, pl.ds(at, 256)] = part.astype(BF16)
            return carry

        lax.fori_loop(0, FEATURES // 256, tile, 0)
        for k in (2, 1, 3):
            px_copy(j, k).start()

    def pz_copy(j):
        return remote(z_send.at[j], z_in.at[j], pz_s.at[j], pz_r.at[j], zpeer)

    def pre_reduce(j):
        for k in (1, 3, 2):
            px_copy(j, k).wait_recv()
        for keep in (0, 1):
            first = (1 - zh if keep == 0 else zh) * 16
            total = pre_f32[j, pl.ds(pl.multiple_of(x * 32 + first, 16), 16), :]
            for k in range(3):
                total = total + pre_in[j, k, pl.ds(pl.multiple_of(first, 16), 16), :].astype(F32)
            if keep == 0:
                z_send[j] = total.astype(BF16)
                pz_copy(j).start()
            else:
                z_own[j] = total

    def owned(j):
        return blocks_of(j) + 2 * x + zh

    def passed(j):
        return blocks_of(j) + 2 * x + (1 - zh)

    def az_copy(j):
        return remote(act.at[owned(j)], act.at[owned(j)], az_s.at[j], az_r.at[j], zpeer)

    def ax_copy(j, k, second):
        block = passed(j) if second else owned(j)
        at = second * 3 + k - 1
        return remote(act.at[block], act.at[block], ax_s.at[j, at], ax_r.at[j, at], xpeer(k))

    def activate(j):
        pz_copy(j).wait_recv()
        pre = z_own[j] + z_in[j].astype(F32) + bias_ref[...]
        act[owned(j)] = jnp.maximum(pre, 0.0).astype(BF16)
        az_copy(j).start()
        for k in (2, 1, 3):
            ax_copy(j, k, 0).start()

    def pass_on(j):
        az_copy(j).wait_recv()
        for k in (2, 1, 3):
            ax_copy(j, k, 1).start()

    def guz_copy():
        return remote(gu_zsend, gu_zin, guz_s.at[0], guz_r.at[0], zpeer)

    def gu_reduce():
        for k in (1, 3, 2):
            gux_copy(k).wait_recv()
        for keep in (0, 1):
            first = (1 - zh if keep == 0 else zh) * 32
            mine = pl.ds(pl.multiple_of(x * 64 + first, 32), 32)
            total = gu_own[mine, :]
            for k in range(3):
                total = total + gu_in[k, pl.ds(pl.multiple_of(first, 32), 32), :]
            if keep == 0:
                gu_zsend[...] = total
                guz_copy().start()
            else:
                gu_own[mine, :] = total

    def hz_copy():
        return remote(hid.at[2 * x + zh], hid.at[2 * x + zh], hz_s.at[0], hz_r.at[0], zpeer)

    def hx_copy(k, second):
        part = 2 * x + ((1 - zh) if second else zh)
        at = second * 3 + k - 1
        return remote(hid.at[part], hid.at[part], hx_s.at[at], hx_r.at[at], xpeer(k))

    def gu_activate():
        guz_copy().wait_recv()
        mine = pl.ds(pl.multiple_of(x * 64 + zh * 32, 32), 32)
        total = gu_own[mine, :] + gu_zin[...]
        gate, up = total[:, :HIDDEN], total[:, HIDDEN:]
        hid[2 * x + zh] = (gate / (1.0 + jnp.exp(-gate)) * up).astype(BF16)
        hz_copy().start()
        for k in (2, 1, 3):
            hx_copy(k, 0).start()

    def gu_pass_on():
        hz_copy().wait_recv()
        for k in (2, 1, 3):
            hx_copy(k, 1).start()

    def out_copy(k):
        there = (e + k) % EXPERTS
        return remote(
            out_send.at[there],
            out_in.at[e],
            out_s.at[k],
            out_r.at[k],
            {"exp": there, "feat": f},
        )

    def down():
        for second in (0, 1):
            for k in (1, 3, 2):
                hx_copy(k, second).wait_recv()
        hidden = hid[...].reshape(EXPERTS * SLOT, HIDDEN)
        for n in range(7):
            cols = pl.ds(n * 128, 128)
            out_send[:, :, cols] = (
                dot(hidden, down_w[:, cols]).reshape(EXPERTS, SLOT, 128).astype(BF16)
            )
        out_in[e] = out_send[e]

        def start(k, carry):
            out_copy(k).start()
            return carry

        lax.fori_loop(1, EXPERTS, start, 0)

    def cm_copy(j):
        return remote(rec.at[j, 1 - core], mate_in.at[j], cm_s.at[j], cm_r.at[j], mate)

    def decode(j):
        for second in (0, 1):
            for k in (1, 3, 2):
                ax_copy(j, k, second).wait_recv()
        rows = act[pl.ds(blocks_of(j), 8)].reshape(CHUNK_ROWS, FEATURES)

        def tile(n, carry):
            at = pl.multiple_of(n * 256, 256)
            part = dot(rows, dec_w[:, pl.ds(at, 256)]).reshape(4, 2, ROWS, 256)
            for c in (0, 1):
                rec[j, c, :, :, pl.ds(at, 256)] = part[:, c]
            return carry

        lax.fori_loop(0, WIDE // 256, tile, 0)
        cm_copy(j).start()

    def fin_copy(j, k):
        there = ((y + 1 + j) % 4) * 4 + (zl + k) % 4
        at = ((1 + j) % 4) * 4 + k
        return remote(
            fin_send.at[j, k],
            fin_in.at[at],
            fin_s.at[at],
            fin_r.at[at],
            {"exp": there * 2 + core, "feat": f},
        )

    def finish(j):
        cm_copy(j).wait_recv()
        for k in range(4):
            to = (zl + k) % 4
            total = rec[j, core, to] + mate_in[j, to]
            if j == CHUNKS - 1 and k == 0:
                fin_own[...] = total
            else:
                fin_send[j, k] = total.astype(BF16)
                fin_copy(j, k).start()

    def row_mate_copy():
        return remote(row_own, row_mate, rm_s.at[0], rm_r.at[0], mate)

    def same_core(there_y, there_z):
        return {"exp": (there_y * 4 + there_z) * 2 + core, "feat": f}

    def row_y_copy(k):
        there = (y + k) % 4
        return remote(
            row_part.at[there], row_in.at[k - 1], ry_s.at[k - 1], ry_r.at[k - 1], same_core(there, zl)
        )

    def row_z_copy(k):
        return remote(
            row_sum, row_zin.at[k - 1], rz_s.at[k - 1], rz_r.at[k - 1], same_core(y, (zl + k) % 4)
        )

    def row_gather_copy(k):
        return remote(
            rows_dec.at[y], rows_dec.at[y], rg_s.at[k - 1], rg_r.at[k - 1], same_core((y + k) % 4, zl)
        )

    def rows_start():
        mine = lax.dot_general(
            dec_w[:, pl.ds(WIDTH, EXTRA)],
            dec_w[:, pl.ds(0, WIDTH)],
            (((0,), (0,)), ((), ())),
            preferred_element_type=F32,
        )
        row_own[...] = mine[:64].astype(BF16).reshape(4, ROWS, WIDTH)
        row_mate_copy().start()

    def rows_y():
        row_mate_copy().wait_recv()
        row_part[...] = (row_own[...].astype(F32) + row_mate[...].astype(F32)).astype(BF16)
        for k in range(1, 4):
            row_y_copy(k).start()

    def rows_z():
        total = row_part[y].astype(F32)
        for k in range(1, 4):
            row_y_copy(k).wait_recv()
            total = total + row_in[k - 1].astype(F32)
        row_sum[...] = total.astype(BF16)
        for k in range(1, 4):
            row_z_copy(k).start()

    def rows_gather():
        total = row_sum[...].astype(F32)
        for k in range(1, 4):
            row_z_copy(k).wait_recv()
            total = total + row_zin[k - 1].astype(F32)
        rows_dec[y] = total.astype(BF16)
        for k in range(1, 4):
            row_gather_copy(k).start()

    pre_multiply(0)
    pre_multiply(1)
    pre_multiply(2)
    pre_multiply(3)
    loads[4].wait()
    rows_start()
    gu_reduce()
    rows_y()
    pre_reduce(0)
    loads[3].wait()
    gu_activate()
    rows_z()
    pre_reduce(1)
    activate(0)
    gu_pass_on()
    pre_reduce(2)
    activate(1)
    pass_on(0)
    pre_reduce(3)
    rows_gather()
    down()
    activate(2)
    pass_on(1)
    decode(0)
    activate(3)
    pass_on(2)
    finish(0)
    decode(1)
    pass_on(3)
    finish(1)
    decode(2)

    def out_arrived(k, carry):
        out_copy(k).wait_recv()
        return carry

    lax.fori_loop(1, EXPERTS, out_arrived, 0)
    for n in range(7):
        cols = pl.ds(n * 128, 128)
        rows = out_in[:, :, cols].astype(F32).reshape(EXPERTS * SLOT, 128).astype(BF16)
        moe_ref[:, cols] = dot(combine[2], rows) + dot(combine[1], rows) + dot(combine[0], rows)
    finish(2)
    decode(3)
    finish(3)

    total = fin_own[...]
    for at in range(1, CHIPS):
        j, k = (at // 4 + 3) % 4, at % 4
        fin_copy(j, k).wait_recv()
        total = total + fin_in[at].astype(F32)
    err_ref[...] = moe_ref[...] - total[:, :WIDTH] - dbias_ref[...]
    for k in range(1, 4):
        row_gather_copy(k).wait_recv()
    change = values_ref[...].astype(F32) - total[:, WIDTH : WIDTH + 64]
    listed = rows_dec[...].reshape(64, WIDTH)
    high, middle, low = three(change)
    steered_ref[...] = moe_ref[...] + (dot(low, listed) + dot(middle, listed) + dot(high, listed))

    def tokens_left(k, carry):
        token_copy(k).wait_send()
        return carry

    lax.fori_loop(1, CHIPS, tokens_left, 0)

    def passes_left(k, carry):
        token_pass(k).wait_send()
        return carry

    lax.fori_loop(0, CHIPS, passes_left, 0)

    def outs_left(k, carry):
        out_copy(k).wait_send()
        return carry

    lax.fori_loop(1, EXPERTS, outs_left, 0)
    guz_copy().wait_send()
    hz_copy().wait_send()
    row_mate_copy().wait_send()
    for k in range(1, 4):
        row_y_copy(k).wait_send()
        row_z_copy(k).wait_send()
        row_gather_copy(k).wait_send()
        gux_copy(k).wait_send()
        hx_copy(k, 0).wait_send()
        hx_copy(k, 1).wait_send()
    for j in range(CHUNKS):
        pz_copy(j).wait_send()
        az_copy(j).wait_send()
        cm_copy(j).wait_send()
        for k in range(1, 4):
            px_copy(j, k).wait_send()
            ax_copy(j, k, 0).wait_send()
            ax_copy(j, k, 1).wait_send()
        for k in range(4):
            if not (j == CHUNKS - 1 and k == 0):
                fin_copy(j, k).wait_send()


def fused(*operands):
    vmem = pl.BlockSpec(memory_space=pltpu.VMEM)
    hbm = pl.BlockSpec(memory_space=pl.ANY)
    dma = pltpu.SemaphoreType.DMA
    scratch = [
        pltpu.VMEM((WIDTH, HIDDEN), BF16),
        pltpu.VMEM((WIDTH, HIDDEN), BF16),
        pltpu.VMEM((HIDDEN, WIDTH), BF16),
        pltpu.VMEM((WIDTH, FEATURES), BF16),
        pltpu.VMEM((FEATURES, WIDE), BF16),
        pltpu.VMEM((EXPERTS, ROWS, WIDE), BF16),
        pltpu.VMEM((EXPERTS * SLOT, 2 * HIDDEN), F32),
        pltpu.VMEM((3, 64, 2 * HIDDEN), F32),
        pltpu.VMEM((32, 2 * HIDDEN), F32),
        pltpu.VMEM((32, 2 * HIDDEN), F32),
        pltpu.VMEM((CHUNKS, CHUNK_ROWS, FEATURES), F32),
        pltpu.VMEM((CHUNKS, CHUNK_ROWS, FEATURES), BF16),
        pltpu.VMEM((CHUNKS, 3, 32, FEATURES), BF16),
        pltpu.VMEM((CHUNKS, ROWS, FEATURES), BF16),
        pltpu.VMEM((CHUNKS, ROWS, FEATURES), BF16),
        pltpu.VMEM((CHUNKS, ROWS, FEATURES), F32),
        pltpu.VMEM((EXPERTS, ROWS, FEATURES), BF16),
        pltpu.VMEM((8, 32, HIDDEN), BF16),
        pltpu.VMEM((EXPERTS, SLOT, WIDTH), BF16),
        pltpu.VMEM((EXPERTS, SLOT, WIDTH), BF16),
        pltpu.VMEM((CHUNKS, 2, 4, ROWS, WIDE), F32),
        pltpu.VMEM((CHUNKS, 4, ROWS, WIDE), F32),
        pltpu.VMEM((CHUNKS, 4, ROWS, WIDE), BF16),
        pltpu.VMEM((CHIPS, ROWS, WIDE), BF16),
        pltpu.VMEM((ROWS, WIDE), F32),
        pltpu.VMEM((3, ROWS, EXPERTS * SLOT), BF16),
        pltpu.VMEM((ROWS, WIDTH), F32),
        pltpu.VMEM((4, ROWS, WIDTH), BF16),
        pltpu.VMEM((4, ROWS, WIDTH), BF16),
        pltpu.VMEM((4, ROWS, WIDTH), BF16),
        pltpu.VMEM((3, ROWS, WIDTH), BF16),
        pltpu.VMEM((ROWS, WIDTH), BF16),
        pltpu.VMEM((3, ROWS, WIDTH), BF16),
        pltpu.VMEM((4, ROWS, WIDTH), BF16),
        dma((5,)),
        dma((CHIPS,)),
        dma((CHIPS,)),
        dma((CHIPS,)),
        dma((CHIPS,)),
        dma((3,)),
        dma((3,)),
        dma((1,)),
        dma((1,)),
        dma((1,)),
        dma((1,)),
        dma((6,)),
        dma((6,)),
        dma((CHUNKS, 3)),
        dma((CHUNKS, 3)),
        dma((CHUNKS,)),
        dma((CHUNKS,)),
        dma((CHUNKS,)),
        dma((CHUNKS,)),
        dma((CHUNKS, 6)),
        dma((CHUNKS, 6)),
        dma((EXPERTS,)),
        dma((EXPERTS,)),
        dma((CHUNKS,)),
        dma((CHUNKS,)),
        dma((CHIPS,)),
        dma((CHIPS,)),
        dma((1,)),
        dma((1,)),
        dma((3,)),
        dma((3,)),
        dma((3,)),
        dma((3,)),
        dma((3,)),
        dma((3,)),
    ]
    return pl.pallas_call(
        kernel,
        out_shape=(
            jax.ShapeDtypeStruct((ROWS, WIDTH), F32),
            jax.ShapeDtypeStruct((ROWS, WIDTH), F32),
        ),
        in_specs=[vmem] * 7 + [hbm] * 5,
        out_specs=(vmem, vmem),
        scratch_shapes=scratch,
        name="fused_layer",
        cost_estimate=pl.CostEstimate(
            flops=6_000_000_000, bytes_accessed=400_000_000, transcendentals=0
        ),
        compiler_params=pltpu.CompilerParams(
            collective_id=0, has_side_effects=True, vmem_limit_bytes=56 << 20
        ),
    )(*operands)


def local(
    tokens,
    route_ids,
    route_weights,
    gate_proj,
    up_proj,
    down_proj,
    enc_weight,
    enc_bias,
    dec_weight,
    dec_bias,
    clamp_ids,
    clamp_values,
):
    ids = jnp.pad(clamp_ids, (0, EXTRA - clamp_ids.shape[0]), constant_values=-1)
    return fused(
        tokens,
        route_ids,
        route_weights,
        enc_bias[None, :],
        dec_bias[None, :],
        ids[None, :],
        clamp_values[None, :],
        gate_proj,
        up_proj,
        down_proj,
        enc_weight,
        dec_weight,
    )


def solution(mesh):
    placed = (
        P("exp", "feat"),
        P("exp", None),
        P("exp", None),
        P("exp", "feat", None),
        P("exp", "feat", None),
        P("exp", None, "feat"),
        P("feat", "exp"),
        P("exp"),
        P("exp", "feat"),
        P("feat"),
        P(),
        P(),
    )
    return jax.shard_map(
        local,
        mesh=mesh,
        in_specs=placed,
        out_specs=(P("exp", "feat"), P("exp", "feat")),
        check_vma=False,
    )
```

time: 526 us -> 133 us (0.25)
  waiting for transfers between devices: 400 us -> 0 us
  Pallas kernels: 0 us -> 124 us
  blocking collectives: 48.5 us -> 0 us
  matrix products: 24 us -> 0 us
  starting transfers between devices: 15.4 us -> 0 us
  between operations: 14.2 us -> 0.64 us
  other arithmetic: 6.81 us -> 0 us
    psum x1 -> x0, waiting for transfers between devices: 267 us -> none  [local(): lax.psum((partial_pre, gate_part, up_part), 'feat')]
    pallas_call x0 -> x1, Pallas kernels: none -> 124 us  [fused(): pl.pallas_call(kernel, out_shape=(jax.ShapeDtypeStruct((ROWS, WIDTH), F32...]
    reduce_scatter x1 -> x0, waiting for transfers between devices: 114 us -> none  [local(): lax.psum_scatter(jnp.concatenate([rebuilt_rows, shift_part], axis=1), 'ex...]
    all_gather x1 -> x0, blocking collectives: 48.5 us -> none  [local(): lax.all_gather(tokens, 'exp', axis=0, tiled=True)]
    dot_general x8 -> x0, matrix products: 24 us -> none  [the longest x1 6.35 us: local(): jnp.dot(lax.all_gather(tokens, 'exp', axis=0, tiled=True), enc_weight, pr...]
    all_to_all x2 -> x0, waiting for transfers between devices: 18.7 us -> none  [the longest x1 18.7 us: local(): lax.all_to_all(expert_out.reshape(expert_count, SLOT, shard_width), 'exp'...]
    all_to_all x2 -> x0, starting transfers between devices: 15.3 us -> none  [the longest x1 10.2 us: local(): lax.all_to_all(outgoing.reshape(expert_count, SLOT, shard_width), 'exp',...]
    gather x2 -> x0, local copies, waits for them, and re-layouts: 5.87 us -> none  [the longest x1 3.3 us: local(): rows_dec = jnp.take(dec_weight, safe_ids, axis=0).astype(jnp.float32)]
  transfers between devices with their start and end apart: 4 -> 0, of which waited for: 3 -> 0; matrix products, arithmetic and copies ran while one was open for 3% -> 0% of each run, Pallas kernels for 0% -> 0%
where the time goes in v1:
time: 133 us; the launch traced here: 132 us
  Pallas kernels  124 us (93%)
  local copies, waits for them, and re-layouts  8.1 us (6%)
    pallas_call x1, Pallas kernels, fused(): pl.pallas_call(kernel, out_shape=(jax.ShapeDtypeStruct((ROWS, WIDTH), F32...  124 us
    unnamed x4, local copies, waits for them, and re-layouts  5.6 us

profile of v1, /device:TPU:1, one launch (start us, length us, event | category | flops | bytes accessed | tf_op | source)
XLA Modules:
  0.0 132.3 jit_solution(11352235695208649305)
XLA Ops:
  0.6 1.2 pad_bitcast_fusion.ids_ref
  1.8 1.3 broadcast_in_dim.13.dbias_ref
  3.1 1.4 %copy.14.route_ref = s32[16,8]{1,0:T(8,128)} copy(s32[16,8]{0,1:T(8,128)} %param.13) | data formatting | bytes 1024 | tf_op args[1]
  4.5 1.4 %copy.15.weight_ref = f32[16,8]{1,0:T(8,128)} copy(f32[16,8]{0,1:T(8,128)} %param.14) | data formatting | bytes 1024 | tf_op args[2]
  5.8 123.6 %fused_layer.1 = (f32[16,896]{1,0:T(8,128)}, f32[16,896]{1,0:T(8,128)}) custom-call(bf16[16,896]{1,0:T(8,128)(2,1)} %tok_ref.1, s32[16,8]{1,0:T(8,128)} %copy.14.route_ref, f32[16,8]{1,0:T(8,128)} %copy.15.weight_ref, f32[1,2048]{1,0:T(1,128)} %bitcast.4, f32[1,896]{1,0:T(1,128)} %broadcast_in_dim.13.dbias_ref, s32[1,128]{1,0:T(1,128)} %pad_bitcast_fusion.ids_ref, ...), custom_call_target="tpu_custom_call" | custom-call | flops 6000000000 | bytes 400000000 | tf_op jit(solution)/shard_map/fused_layer/pallas_call | solution.py:672
  129.4 1.4 %copy.18 = f32[16,896]{1,0:T(8,128)} copy(f32[16,896]{1,0:T(8,128)} %get-tuple-element.4) | data formatting | bytes 114688
  130.9 1.4 %copy.19 = f32[16,896]{1,0:T(8,128)} copy(f32[16,896]{1,0:T(8,128)} %get-tuple-element.5) | data formatting | bytes 114688

commit v2 on v1

v2 whole, which is shorter than its diff:
```python
import functools

import jax
import jax.numpy as jnp
from jax import lax
from jax.experimental import pallas as pl
from jax.experimental.pallas import tpu as pltpu
from jax.sharding import PartitionSpec as P

SLOT = 8
ROWS = 16
WIDTH = 896
EXTRA = 128
WIDE = WIDTH + EXTRA
FEATURES = 2048
HIDDEN = 1024
CHIPS = 16
EXPERTS = 32
CHUNKS = 4
CHUNK_ROWS = 128
MESH = pl.DeviceIdType.MESH
F32 = jnp.float32
BF16 = jnp.bfloat16


def remote(src, dst, send_sem, recv_sem, device):
    return pltpu.make_async_remote_copy(
        src_ref=src,
        dst_ref=dst,
        send_sem=send_sem,
        recv_sem=recv_sem,
        device_id=device,
        device_id_type=MESH,
    )


def dot(a, b):
    return jnp.dot(a, b, preferred_element_type=F32)


def kernel(
    tok_ref,
    route_ref,
    weight_ref,
    bias_ref,
    ids_ref,
    values_ref,
    gate_hbm,
    up_hbm,
    down_hbm,
    enc_hbm,
    dec_hbm,
    recon_ref,
    moe_ref,
    shift_ref,
    gate_w,
    up_w,
    down_w,
    enc_w,
    dec_w,
    tok_all,
    gu_own,
    gu_ring,
    gu_in,
    gu_zsend,
    gu_zin,
    pre_f32,
    pre_send,
    pre_ring,
    pre_in,
    z_send,
    z_in,
    z_own,
    act,
    hid,
    out_send,
    out_in,
    rec,
    mate_in,
    fin_send,
    fin_in,
    fin_own,
    combine,
    row_own,
    row_mate,
    row_part,
    row_in,
    row_sum,
    row_zin,
    rows_dec,
    load_sem,
    tz_s,
    tz_r,
    ty_s,
    ty_r,
    mate_s,
    mate_r,
    gux_s,
    gux_r,
    guz_s,
    guz_r,
    hz_s,
    hz_r,
    hx_s,
    hx_r,
    px_s,
    px_r,
    pz_s,
    pz_r,
    az_s,
    az_r,
    ax_s,
    ax_r,
    out_s,
    out_r,
    cm_s,
    cm_r,
    fin_s,
    fin_r,
    rm_s,
    rm_r,
    ry_s,
    ry_r,
    rz_s,
    rz_r,
    rg_s,
    rg_r,
):
    e = lax.axis_index("exp")
    f = lax.axis_index("feat")
    chip, core = e // 2, e % 2
    y, zl = chip // 4, chip % 4
    zh, x = f // 4, f % 4
    mate = {"exp": chip * 2 + (1 - core), "feat": f}
    zpeer = {"exp": e, "feat": (1 - zh) * 4 + x}

    def xpeer(k):
        return {"exp": e, "feat": zh * 4 + (x + k) % 4}

    load_enc = pltpu.make_async_copy(enc_hbm, enc_w, load_sem.at[0])
    load_gate = pltpu.make_async_copy(gate_hbm.at[0], gate_w, load_sem.at[1])
    load_up = pltpu.make_async_copy(up_hbm.at[0], up_w, load_sem.at[2])
    load_dec = pltpu.make_async_copy(dec_hbm, dec_w.at[:, pl.ds(0, WIDTH)], load_sem.at[3])
    load_down = pltpu.make_async_copy(down_hbm.at[0], down_w, load_sem.at[4])
    for load in (load_enc, load_gate, load_up, load_dec, load_down):
        load.start()

    barrier = pltpu.get_barrier_semaphore()

    def greet(k, carry):
        pl.semaphore_signal(
            barrier, inc=1, device_id={"exp": (e + k) % EXPERTS, "feat": f}, device_id_type=MESH
        )
        return carry

    lax.fori_loop(1, EXPERTS, greet, 0)
    for k in range(1, 4):
        pl.semaphore_signal(barrier, inc=1, device_id=xpeer(k), device_id_type=MESH)
    pl.semaphore_signal(barrier, inc=1, device_id=zpeer, device_id_type=MESH)
    expert_of = lax.broadcasted_iota(jnp.int32, (EXTRA, ROWS), 0)
    named = jnp.zeros((EXTRA, ROWS), F32)
    spread = jnp.zeros((EXTRA, ROWS), F32)
    for k in range(route_ref.shape[0]):
        hit = route_ref[k : k + 1, :] == expert_of
        named = jnp.where(hit, 1.0, named)
        spread = jnp.where(hit, weight_ref[k : k + 1, :], spread)
    one = lax.broadcasted_iota(jnp.int32, (ROWS, ROWS), 0)
    other = lax.broadcasted_iota(jnp.int32, (ROWS, ROWS), 1)
    before = dot(named.astype(BF16), jnp.where(one < other, 1.0, 0.0).astype(BF16))
    code_t = jnp.where((named > 0) & (before < SLOT), before + 1.0, 0.0).astype(BF16)
    code = lax.dot_general(
        jnp.where(one == other, 1.0, 0.0).astype(BF16),
        code_t,
        (((1,), (1,)), ((), ())),
        preferred_element_type=F32,
    ).astype(BF16)
    tok_all[e, :, pl.ds(0, WIDTH)] = tok_ref[...]
    tok_all[e, :, pl.ds(WIDTH, EXTRA)] = code
    pl.semaphore_wait(barrier, EXPERTS - 1 + 4)

    def same_core(there_y, there_z):
        return {"exp": (there_y * 4 + there_z) * 2 + core, "feat": f}

    def block_at(back_y, back_z, which):
        return (((y + 4 - back_y) % 4) * 4 + (zl + 4 - back_z) % 4) * 2 + which

    def token_z(k):
        return remote(
            tok_all.at[e], tok_all.at[e], tz_s.at[k - 1], tz_r.at[k - 1], same_core(y, (zl + k) % 4)
        )

    def token_z_arrival(k):
        block = block_at(0, k, core)
        return remote(tok_all.at[block], tok_all.at[block], tz_s.at[k - 1], tz_r.at[k - 1], mate)

    def token_y(k, m):
        block = block_at(0, m, core)
        at = (k - 1) * 4 + m
        return remote(
            tok_all.at[block], tok_all.at[block], ty_s.at[at], ty_r.at[at], same_core((y + k) % 4, zl)
        )

    def token_y_arrival(k, m):
        block = block_at(k, m, core)
        at = (k - 1) * 4 + m
        return remote(tok_all.at[block], tok_all.at[block], ty_s.at[at], ty_r.at[at], mate)

    def token_pass(k, m):
        block = block_at(k, m, core)
        at = k * 4 + m
        return remote(tok_all.at[block], tok_all.at[block], mate_s.at[at], mate_r.at[at], mate)

    def token_pass_arrival(k, m):
        block = block_at(k, m, 1 - core)
        at = k * 4 + m
        return remote(tok_all.at[block], tok_all.at[block], mate_s.at[at], mate_r.at[at], mate)

    for k in (1, 3, 2):
        token_z(k).start()
    token_pass(0, 0).start()
    for k in (2, 1, 3):
        token_y(k, 0).start()
    for m in (1, 3, 2):
        token_z_arrival(m).wait_recv()
        token_pass(0, m).start()
        for k in (2, 1, 3):
            token_y(k, m).start()

    def from_y(k):
        for m in (0, 1, 3, 2):
            token_y_arrival(k, m).wait_recv()
            token_pass(k, m).start()

    def from_mate(k):
        for m in (0, 1, 3, 2):
            token_pass_arrival(k, m).wait_recv()

    slot_lane = lax.broadcasted_iota(jnp.int32, (EXTRA, EXPERTS * SLOT), 1)
    widen = jnp.where(
        (slot_lane >> 3) == lax.broadcasted_iota(jnp.int32, (EXTRA, EXPERTS * SLOT), 0), 1.0, 0.0
    ).astype(BF16)
    slot_wanted = (
        (lax.broadcasted_iota(jnp.int32, (ROWS, EXPERTS * SLOT), 1) & 7) + 1
    ).astype(F32)
    in_slot = dot(code, widen) == slot_wanted

    def three(value):
        high = value.astype(BF16)
        rest = value - high.astype(F32)
        middle = rest.astype(BF16)
        return high, middle, (rest - middle.astype(F32)).astype(BF16)

    for part, piece in enumerate(three(spread)):
        widened = lax.dot_general(
            piece, widen, (((0,), (0,)), ((), ())), preferred_element_type=F32
        )
        combine[part] = jnp.where(in_slot, widened, 0.0).astype(BF16)
    clamps = ids_ref.shape[1]
    feature = lax.broadcasted_iota(jnp.int32, (FEATURES, clamps), 0) + e * FEATURES
    listed_col = jnp.where(feature == ids_ref[...], 1.0, 0.0).astype(BF16)
    dec_w[:, pl.ds(WIDTH, EXTRA)] = jnp.concatenate(
        [listed_col, jnp.zeros((FEATURES, EXTRA - clamps), BF16)], axis=1
    )

    toward = (1, 3)

    def quarter(k):
        return (x + k) % 4

    def half_rows(k, half, size):
        return pl.ds(pl.multiple_of(quarter(k) * 2 * size + half * size, size), size)

    def gu_ring_copy(n):
        return remote(
            gu_own.at[half_rows(2, n, 32)],
            gu_ring.at[n],
            gux_s.at[n],
            gux_r.at[n],
            xpeer(toward[n]),
        )

    def gu_early(n):
        return remote(
            gu_own.at[half_rows(toward[n], 1 - n, 32)],
            gu_in.at[1 - n, 0],
            gux_s.at[2 + n],
            gux_r.at[2 + n],
            xpeer(toward[n]),
        )

    def gu_late(n):
        return remote(
            gu_own.at[half_rows(toward[n], n, 32)],
            gu_in.at[n, 1],
            gux_s.at[4 + n],
            gux_r.at[4 + n],
            xpeer(toward[n]),
        )

    def gu_relay():
        for n in (0, 1):
            gu_ring_copy(n).wait_recv()
            rows = half_rows(toward[n], n, 32)
            gu_own[rows, :] = gu_own[rows, :] + gu_ring[n]
            gu_late(n).start()

    def gu_multiply():
        everything = tok_all[...].reshape(EXPERTS * ROWS, WIDE)
        pick = jnp.where(lax.broadcasted_iota(jnp.int32, (8, EXTRA), 1) == e, 1.0, 0.0).astype(BF16)
        codes = lax.dot_general(
            pick, everything[:, WIDTH:], (((1,), (1,)), ((), ())), preferred_element_type=F32
        )
        slot_row = lax.broadcasted_iota(jnp.int32, (EXPERTS * SLOT, EXPERTS * ROWS), 0)
        token_col = lax.broadcasted_iota(jnp.int32, (EXPERTS * SLOT, EXPERTS * ROWS), 1)
        same_block = (slot_row >> 3) == (token_col >> 4)
        wanted = ((slot_row & 7) + 1).astype(F32)
        picker = jnp.where(same_block & (codes[0:1, :] == wanted), 1.0, 0.0).astype(BF16)
        expert_in = dot(picker, everything[:, :WIDTH]).astype(BF16)

        load_gate.wait()
        load_up.wait()
        for half, weights in ((0, gate_w), (1, up_w)):

            def gate_tile(n, carry, half=half, weights=weights):
                at = pl.multiple_of(n * 256, 256)
                gu_own[:, pl.ds(pl.multiple_of(half * HIDDEN + n * 256, 256), 256)] = dot(
                    expert_in, weights[:, pl.ds(at, 256)]
                )
                return carry

            lax.fori_loop(0, HIDDEN // 256, gate_tile, 0)
        for n in (0, 1):
            gu_ring_copy(n).start()
        for n in (0, 1):
            gu_early(n).start()

    def blocks_of(j):
        return ((y + j) % 4) * 8

    def pre_ring_copy(j, n):
        return remote(
            pre_send.at[j, half_rows(2, n, 16)],
            pre_ring.at[j, n],
            px_s.at[j, n],
            px_r.at[j, n],
            xpeer(toward[n]),
        )

    def pre_early(j, n):
        return remote(
            pre_send.at[j, half_rows(toward[n], 1 - n, 16)],
            pre_in.at[j, 1 - n, 0],
            px_s.at[j, 2 + n],
            px_r.at[j, 2 + n],
            xpeer(toward[n]),
        )

    def pre_late(j, n):
        return remote(
            pre_send.at[j, half_rows(toward[n], n, 16)],
            pre_in.at[j, n, 1],
            px_s.at[j, 4 + n],
            px_r.at[j, 4 + n],
            xpeer(toward[n]),
        )

    def pre_relay(j):
        for n in (0, 1):
            pre_ring_copy(j, n).wait_recv()
            rows = half_rows(toward[n], n, 16)
            pre_send[j, rows, :] = (pre_f32[j, rows, :] + pre_ring[j, n].astype(F32)).astype(BF16)
            pre_late(j, n).start()

    def pre_multiply(j):
        rows = tok_all[pl.ds(blocks_of(j), 8)].reshape(CHUNK_ROWS, WIDE)[:, :WIDTH]

        def tile(n, carry):
            at = pl.multiple_of(n * 256, 256)
            part = dot(rows, enc_w[:, pl.ds(at, 256)])
            pre_f32[j, :, pl.ds(at, 256)] = part
            pre_send[j, :, pl.ds(at, 256)] = part.astype(BF16)
            return carry

        lax.fori_loop(0, FEATURES // 256, tile, 0)
        for n in (0, 1):
            pre_ring_copy(j, n).start()
        for n in (0, 1):
            pre_early(j, n).start()

    def pz_copy(j):
        return remote(z_send.at[j], z_in.at[j], pz_s.at[j], pz_r.at[j], zpeer)

    def pre_reduce(j):
        for n in (0, 1):
            pre_early(j, n).wait_recv()
            pre_late(j, n).wait_recv()
        for keep in (0, 1):
            half = 1 - zh if keep == 0 else zh
            total = pre_f32[j, half_rows(0, half, 16), :]
            for k in range(2):
                total = total + pre_in[j, half, k].astype(F32)
            if keep == 0:
                z_send[j] = total.astype(BF16)
                pz_copy(j).start()
            else:
                z_own[j] = total

    def owned(j):
        return blocks_of(j) + 2 * x + zh

    def passed(j):
        return blocks_of(j) + 2 * x + (1 - zh)

    def az_copy(j):
        return remote(act.at[owned(j)], act.at[owned(j)], az_s.at[j], az_r.at[j], zpeer)

    def block_of(j, k, side):
        return blocks_of(j) + 2 * quarter(k) + side

    def ax_copy(j, n, second):
        block = passed(j) if second else owned(j)
        at = second * 2 + n
        return remote(act.at[block], act.at[block], ax_s.at[j, at], ax_r.at[j, at], xpeer(toward[n]))

    def ax_relay(j, n):
        block = block_of(j, toward[1 - n], zh if n == 0 else 1 - zh)
        return remote(
            act.at[block], act.at[block], ax_s.at[j, 4 + n], ax_r.at[j, 4 + n], xpeer(toward[n])
        )

    def activate(j):
        pz_copy(j).wait_recv()
        pre = z_own[j] + z_in[j].astype(F32) + bias_ref[...]
        act[owned(j)] = jnp.maximum(pre, 0.0).astype(BF16)
        az_copy(j).start()
        for n in (0, 1):
            ax_copy(j, n, 0).start()

    def pass_on(j):
        az_copy(j).wait_recv()
        for n in (1, 0):
            ax_copy(j, n, 1).start()

    def relay(j):
        ax_copy(j, 0, 0).wait_recv()
        ax_relay(j, 0).start()
        ax_copy(j, 1, 1).wait_recv()
        ax_relay(j, 1).start()

    def guz_copy():
        return remote(gu_zsend, gu_zin, guz_s.at[0], guz_r.at[0], zpeer)

    def gu_reduce():
        for n in (0, 1):
            gu_early(n).wait_recv()
            gu_late(n).wait_recv()
        for keep in (0, 1):
            half = 1 - zh if keep == 0 else zh
            mine = half_rows(0, half, 32)
            total = gu_own[mine, :] + gu_in[half, 0] + gu_in[half, 1]
            if keep == 0:
                gu_zsend[...] = total
                guz_copy().start()
            else:
                gu_own[mine, :] = total

    def hz_copy():
        return remote(hid.at[2 * x + zh], hid.at[2 * x + zh], hz_s.at[0], hz_r.at[0], zpeer)

    def hx_copy(n, second):
        part = 2 * x + ((1 - zh) if second else zh)
        at = second * 2 + n
        return remote(hid.at[part], hid.at[part], hx_s.at[at], hx_r.at[at], xpeer(toward[n]))

    def hx_relay(n):
        part = 2 * quarter(toward[1 - n]) + (zh if n == 0 else 1 - zh)
        return remote(hid.at[part], hid.at[part], hx_s.at[4 + n], hx_r.at[4 + n], xpeer(toward[n]))

    def gu_activate():
        guz_copy().wait_recv()
        total = gu_own[half_rows(0, zh, 32), :] + gu_zin[...]
        gate, up = total[:, :HIDDEN], total[:, HIDDEN:]
        hid[2 * x + zh] = (gate / (1.0 + jnp.exp(-gate)) * up).astype(BF16)
        hz_copy().start()
        for n in (0, 1):
            hx_copy(n, 0).start()

    def gu_pass_on():
        hz_copy().wait_recv()
        for n in (1, 0):
            hx_copy(n, 1).start()

    def hid_relay():
        hx_copy(0, 0).wait_recv()
        hx_relay(0).start()
        hx_copy(1, 1).wait_recv()
        hx_relay(1).start()

    def out_copy(k):
        there = (e + k) % EXPERTS
        return remote(
            out_send.at[there],
            out_in.at[e],
            out_s.at[k],
            out_r.at[k],
            {"exp": there, "feat": f},
        )

    def down():
        hx_copy(1, 0).wait_recv()
        hx_copy(0, 1).wait_recv()
        hx_relay(0).wait_recv()
        hx_relay(1).wait_recv()
        load_down.wait()
        hidden = hid[...].reshape(EXPERTS * SLOT, HIDDEN)
        for n in range(7):
            cols = pl.ds(n * 128, 128)
            out_send[:, :, cols] = (
                dot(hidden, down_w[:, cols]).reshape(EXPERTS, SLOT, 128).astype(BF16)
            )
        out_in[e] = out_send[e]

        def start(k, carry):
            out_copy(k).start()
            return carry

        lax.fori_loop(1, EXPERTS, start, 0)

    def cm_copy(j):
        return remote(rec.at[j, 1 - core], mate_in.at[j], cm_s.at[j], cm_r.at[j], mate)

    def decode(j):
        ax_copy(j, 1, 0).wait_recv()
        ax_copy(j, 0, 1).wait_recv()
        ax_relay(j, 0).wait_recv()
        ax_relay(j, 1).wait_recv()
        rows = act[pl.ds(blocks_of(j), 8)].reshape(CHUNK_ROWS, FEATURES)

        def tile(n, carry):
            at = pl.multiple_of(n * 256, 256)
            part = dot(rows, dec_w[:, pl.ds(at, 256)]).reshape(4, 2, ROWS, 256)
            for c in (0, 1):
                rec[j, c, :, :, pl.ds(at, 256)] = part[:, c]
            return carry

        lax.fori_loop(0, WIDE // 256, tile, 0)
        cm_copy(j).start()

    def fin_copy(j, k):
        there = ((y + j) % 4) * 4 + (zl + k) % 4
        at = j * 4 + k
        return remote(
            fin_send.at[j, k],
            fin_in.at[at],
            fin_s.at[at],
            fin_r.at[at],
            {"exp": there * 2 + core, "feat": f},
        )

    def finish(j):
        cm_copy(j).wait_recv()
        for k in range(4):
            to = (zl + k) % 4
            total = rec[j, core, to] + mate_in[j, to]
            if j == 0 and k == 0:
                fin_own[...] = total
            else:
                fin_send[j, k] = total.astype(BF16)
                fin_copy(j, k).start()

    def row_mate_copy():
        return remote(row_own, row_mate, rm_s.at[0], rm_r.at[0], mate)

    def row_y_copy(k):
        there = (y + k) % 4
        return remote(
            row_part.at[there], row_in.at[k - 1], ry_s.at[k - 1], ry_r.at[k - 1], same_core(there, zl)
        )

    def row_z_copy(k):
        return remote(
            row_sum, row_zin.at[k - 1], rz_s.at[k - 1], rz_r.at[k - 1], same_core(y, (zl + k) % 4)
        )

    def row_gather_copy(k):
        return remote(
            rows_dec.at[y], rows_dec.at[y], rg_s.at[k - 1], rg_r.at[k - 1], same_core((y + k) % 4, zl)
        )

    def rows_start():
        mine = lax.dot_general(
            dec_w[:, pl.ds(WIDTH, EXTRA)],
            dec_w[:, pl.ds(0, WIDTH)],
            (((0,), (0,)), ((), ())),
            preferred_element_type=F32,
        )
        row_own[...] = mine[:64].astype(BF16).reshape(4, ROWS, WIDTH)
        row_mate_copy().start()

    def rows_y():
        row_mate_copy().wait_recv()
        row_part[...] = (row_own[...].astype(F32) + row_mate[...].astype(F32)).astype(BF16)
        for k in range(1, 4):
            row_y_copy(k).start()

    def rows_z():
        total = row_part[y].astype(F32)
        for k in range(1, 4):
            row_y_copy(k).wait_recv()
            total = total + row_in[k - 1].astype(F32)
        row_sum[...] = total.astype(BF16)
        for k in range(1, 4):
            row_z_copy(k).start()

    def rows_gather():
        total = row_sum[...].astype(F32)
        for k in range(1, 4):
            row_z_copy(k).wait_recv()
            total = total + row_zin[k - 1].astype(F32)
        rows_dec[y] = total.astype(BF16)
        for k in range(1, 4):
            row_gather_copy(k).start()

    from_mate(0)
    load_enc.wait()
    pre_multiply(0)
    for k in (1, 3, 2):
        from_y(k)
    for k in (1, 3, 2):
        from_mate(k)
    gu_multiply()
    pre_relay(0)
    pre_multiply(1)
    pre_reduce(0)
    pre_multiply(2)
    activate(0)
    pre_multiply(3)
    pass_on(0)
    load_dec.wait()
    rows_start()
    gu_relay()
    relay(0)
    pre_relay(1)
    rows_y()
    gu_reduce()
    pre_reduce(1)
    pre_relay(2)
    gu_activate()
    activate(1)
    rows_z()
    pre_reduce(2)
    gu_pass_on()
    pass_on(1)
    pre_relay(3)
    activate(2)
    hid_relay()
    relay(1)
    pre_reduce(3)
    rows_gather()
    pass_on(2)
    down()
    decode(0)
    activate(3)
    finish(0)
    relay(2)
    pass_on(3)
    decode(1)
    finish(1)
    relay(3)
    decode(2)
    finish(2)

    def out_arrived(k, carry):
        out_copy(k).wait_recv()
        return carry

    lax.fori_loop(1, EXPERTS, out_arrived, 0)
    for n in range(7):
        cols = pl.ds(n * 128, 128)
        rows = out_in[:, :, cols].astype(F32).reshape(EXPERTS * SLOT, 128).astype(BF16)
        moe_ref[:, cols] = dot(combine[2], rows) + dot(combine[1], rows) + dot(combine[0], rows)
    decode(3)
    finish(3)

    total = fin_own[...]
    for at in range(1, CHIPS):
        j, k = at // 4, at % 4
        fin_copy(j, k).wait_recv()
        total = total + fin_in[at].astype(F32)
    recon_ref[...] = total[:, :WIDTH]
    for k in range(1, 4):
        row_gather_copy(k).wait_recv()
    change = values_ref[...].astype(F32) - total[:, WIDTH : WIDTH + clamps]
    listed = rows_dec[...].reshape(64, WIDTH)
    high, middle, low = three(change)
    shift_ref[...] = dot(low, listed) + dot(middle, listed) + dot(high, listed)

    for k in range(1, 4):
        token_z(k).wait_send()
        for m in range(4):
            token_y(k, m).wait_send()
    for k in range(4):
        for m in range(4):
            token_pass(k, m).wait_send()

    def outs_left(k, carry):
        out_copy(k).wait_send()
        return carry

    lax.fori_loop(1, EXPERTS, outs_left, 0)
    guz_copy().wait_send()
    hz_copy().wait_send()
    row_mate_copy().wait_send()
    for k in range(1, 4):
        row_y_copy(k).wait_send()
        row_z_copy(k).wait_send()
        row_gather_copy(k).wait_send()
    for n in (0, 1):
        gu_ring_copy(n).wait_send()
        gu_early(n).wait_send()
        gu_late(n).wait_send()
        hx_copy(n, 0).wait_send()
        hx_copy(n, 1).wait_send()
        hx_relay(n).wait_send()
    for j in range(CHUNKS):
        pz_copy(j).wait_send()
        az_copy(j).wait_send()
        cm_copy(j).wait_send()
        for n in (0, 1):
            pre_ring_copy(j, n).wait_send()
            pre_early(j, n).wait_send()
            pre_late(j, n).wait_send()
            ax_copy(j, n, 0).wait_send()
            ax_copy(j, n, 1).wait_send()
            ax_relay(j, n).wait_send()
        for k in range(4):
            if not (j == 0 and k == 0):
                fin_copy(j, k).wait_send()


def fused(*operands):
    vmem = pl.BlockSpec(memory_space=pltpu.VMEM)
    hbm = pl.BlockSpec(memory_space=pl.ANY)
    dma = pltpu.SemaphoreType.DMA
    scratch = [
        pltpu.VMEM((WIDTH, HIDDEN), BF16),
        pltpu.VMEM((WIDTH, HIDDEN), BF16),
        pltpu.VMEM((HIDDEN, WIDTH), BF16),
        pltpu.VMEM((WIDTH, FEATURES), BF16),
        pltpu.VMEM((FEATURES, WIDE), BF16),
        pltpu.VMEM((EXPERTS, ROWS, WIDE), BF16),
        pltpu.VMEM((EXPERTS * SLOT, 2 * HIDDEN), F32),
        pltpu.VMEM((2, 32, 2 * HIDDEN), F32),
        pltpu.VMEM((2, 2, 32, 2 * HIDDEN), F32),
        pltpu.VMEM((32, 2 * HIDDEN), F32),
        pltpu.VMEM((32, 2 * HIDDEN), F32),
        pltpu.VMEM((CHUNKS, CHUNK_ROWS, FEATURES), F32),
        pltpu.VMEM((CHUNKS, CHUNK_ROWS, FEATURES), BF16),
        pltpu.VMEM((CHUNKS, 2, ROWS, FEATURES), BF16),
        pltpu.VMEM((CHUNKS, 2, 2, ROWS, FEATURES), BF16),
        pltpu.VMEM((CHUNKS, ROWS, FEATURES), BF16),
        pltpu.VMEM((CHUNKS, ROWS, FEATURES), BF16),
        pltpu.VMEM((CHUNKS, ROWS, FEATURES), F32),
        pltpu.VMEM((EXPERTS, ROWS, FEATURES), BF16),
        pltpu.VMEM((8, 32, HIDDEN), BF16),
        pltpu.VMEM((EXPERTS, SLOT, WIDTH), BF16),
        pltpu.VMEM((EXPERTS, SLOT, WIDTH), BF16),
        pltpu.VMEM((CHUNKS, 2, 4, ROWS, WIDE), F32),
        pltpu.VMEM((CHUNKS, 4, ROWS, WIDE), F32),
        pltpu.VMEM((CHUNKS, 4, ROWS, WIDE), BF16),
        pltpu.VMEM((CHIPS, ROWS, WIDE), BF16),
        pltpu.VMEM((ROWS, WIDE), F32),
        pltpu.VMEM((3, ROWS, EXPERTS * SLOT), BF16),
        pltpu.VMEM((4, ROWS, WIDTH), BF16),
        pltpu.VMEM((4, ROWS, WIDTH), BF16),
        pltpu.VMEM((4, ROWS, WIDTH), BF16),
        pltpu.VMEM((3, ROWS, WIDTH), BF16),
        pltpu.VMEM((ROWS, WIDTH), BF16),
        pltpu.VMEM((3, ROWS, WIDTH), BF16),
        pltpu.VMEM((4, ROWS, WIDTH), BF16),
        dma((5,)),
        dma((3,)),
        dma((3,)),
        dma((12,)),
        dma((12,)),
        dma((CHIPS,)),
        dma((CHIPS,)),
        dma((6,)),
        dma((6,)),
        dma((1,)),
        dma((1,)),
        dma((1,)),
        dma((1,)),
        dma((6,)),
        dma((6,)),
        dma((CHUNKS, 6)),
        dma((CHUNKS, 6)),
        dma((CHUNKS,)),
        dma((CHUNKS,)),
        dma((CHUNKS,)),
        dma((CHUNKS,)),
        dma((CHUNKS, 6)),
        dma((CHUNKS, 6)),
        dma((EXPERTS,)),
        dma((EXPERTS,)),
        dma((CHUNKS,)),
        dma((CHUNKS,)),
        dma((CHIPS,)),
        dma((CHIPS,)),
        dma((1,)),
        dma((1,)),
        dma((3,)),
        dma((3,)),
        dma((3,)),
        dma((3,)),
        dma((3,)),
        dma((3,)),
    ]
    return pl.pallas_call(
        kernel,
        out_shape=(
            jax.ShapeDtypeStruct((ROWS, WIDTH), F32),
            jax.ShapeDtypeStruct((ROWS, WIDTH), F32),
            jax.ShapeDtypeStruct((ROWS, WIDTH), F32),
        ),
        in_specs=[vmem] * 6 + [hbm] * 5,
        out_specs=(vmem, vmem, vmem),
        scratch_shapes=scratch,
        name="fused_layer",
        cost_estimate=pl.CostEstimate(
            flops=6_000_000_000, bytes_accessed=400_000_000, transcendentals=0
        ),
        compiler_params=pltpu.CompilerParams(
            collective_id=0, has_side_effects=True, vmem_limit_bytes=56 << 20
        ),
    )(*operands)


def local(
    tokens,
    route_ids,
    route_weights,
    gate_proj,
    up_proj,
    down_proj,
    enc_weight,
    enc_bias,
    dec_weight,
    dec_bias,
    clamp_ids,
    clamp_values,
):
    recon, moe_out, shift = fused(
        tokens,
        route_ids.T,
        route_weights.T,
        enc_bias[None, :],
        clamp_ids[None, :],
        clamp_values[None, :],
        gate_proj,
        up_proj,
        down_proj,
        enc_weight,
        dec_weight,
    )
    return moe_out - recon - dec_bias, moe_out + shift


def solution(mesh):
    placed = (
        P("exp", "feat"),
        P("exp", None),
        P("exp", None),
        P("exp", "feat", None),
        P("exp", "feat", None),
        P("exp", None, "feat"),
        P("feat", "exp"),
        P("exp"),
        P("exp", "feat"),
        P("feat"),
        P(),
        P(),
    )
    return jax.shard_map(
        local,
        mesh=mesh,
        in_specs=placed,
        out_specs=(P("exp", "feat"), P("exp", "feat")),
        check_vma=False,
    )
```

time: 133 us -> 132 us (level)
  local copies, waits for them, and re-layouts: 8.1 us -> 0.01 us
  Pallas kernels: 124 us -> 129 us
  other arithmetic: 0 us -> 1.53 us
    unnamed x4 -> x2, local copies, waits for them, and re-layouts: 5.6 us -> 0.01 us
    pallas_call x1, Pallas kernels: 124 us -> 129 us  [fused(): pl.pallas_call(kernel, out_shape=(jax.ShapeDtypeStruct((ROWS, WIDTH), F32...]
    broadcast_in_dim x2 -> x0, local copies, waits for them, and re-layouts: 2.5 us -> none  [the longest x1 1.28 us: local(): dec_bias[None, :]]
    add x0 -> x1, other arithmetic: none -> 1.53 us  [local(): return (moe_out - recon - dec_bias, moe_out + shift)]
where the time goes in v2:
time: 132 us; the launch traced here: 131 us
  Pallas kernels  129 us (98%)
  other arithmetic  1.53 us (1%)
    pallas_call x1, Pallas kernels, fused(): pl.pallas_call(kernel, out_shape=(jax.ShapeDtypeStruct((ROWS, WIDTH), F32...  129 us

profile of v2, /device:TPU:1, one launch (start us, length us, event | category | flops | bytes accessed | tf_op | source)
XLA Modules:
  0.0 131.3 jit_solution(16273876744974373230)
XLA Ops:
  0.6 0.0 copy-start
  0.6 129.1 %fused_layer.1 = (f32[16,896]{1,0:T(8,128)}, f32[16,896]{1,0:T(8,128)}, f32[16,896]{1,0:T(8,128)}) custom-call(bf16[16,896]{1,0:T(8,128)(2,1)} %tok_ref.1, s32[8,16]{1,0:T(8,128)} %bitcast.6, f32[8,16]{1,0:T(8,128)} %bitcast.7, f32[1,2048]{1,0:T(1,128)} %bitcast.5, s32[1,64]{1,0:T(1,128)} %bitcast.8, bf16[1,64]{1,0:T(2,128)(2,1)} %bitcast.9, ...), custom_call_target="tpu_custom_call" | custom-call | flops 6000000000 | bytes 400000000 | tf_op jit(solution)/shard_map/fused_layer/pallas_call | solution.py:819
  129.8 0.0 copy-done
  129.8 1.5 %fusion = (f32[16,896]{1,0:T(8,128)}, f32[16,896]{1,0:T(8,128)}) fusion(f32[16,896]{1,0:T(8,128)} %get-tuple-element.5, f32[16,896]{1,0:T(8,128)} %get-tuple-element.7, f32[896]{0:T(1024)S(1)} %copy-done, f32[16,896]{1,0:T(8,128)} %get-tuple-element.6), kind=kLoop, calls=%fused_computation.1 | loop fusion | flops 43008 | bytes 290304 | tf_op jit(solution)/shard_map/add | solution.py:866
Async XLA Ops:
  0.6 129.2 %copy-start = (f32[896]{0:T(1024)S(1)}, f32[896]{0:T(1024)}, u32[]{:S(2)}) copy-start(f32[896]{0:T(1024)} %param.21) | copy-start | bytes 10756

commit v3 on v2

v3 whole, which is shorter than its diff:
```python
import functools

import jax
import jax.numpy as jnp
from jax import lax
from jax.experimental import pallas as pl
from jax.experimental.pallas import tpu as pltpu
from jax.sharding import PartitionSpec as P

SLOT = 8
ROWS = 16
WIDTH = 896
EXTRA = 128
WIDE = WIDTH + EXTRA
FEATURES = 2048
HIDDEN = 1024
CHIPS = 16
EXPERTS = 32
CHUNKS = 4
CHUNK_ROWS = 128
MESH = pl.DeviceIdType.MESH
F32 = jnp.float32
BF16 = jnp.bfloat16


def remote(src, dst, send_sem, recv_sem, device):
    return pltpu.make_async_remote_copy(
        src_ref=src,
        dst_ref=dst,
        send_sem=send_sem,
        recv_sem=recv_sem,
        device_id=device,
        device_id_type=MESH,
    )


def dot(a, b):
    return jnp.dot(a, b, preferred_element_type=F32)


def kernel(
    tok_hbm,
    route_hbm,
    weight_hbm,
    bias_hbm,
    ids_hbm,
    values_hbm,
    gate_hbm,
    up_hbm,
    down_hbm,
    enc_hbm,
    dec_hbm,
    recon_hbm,
    moe_hbm,
    shift_hbm,
    route_ref,
    weight_ref,
    bias_ref,
    ids_ref,
    values_ref,
    recon_ref,
    moe_ref,
    shift_ref,
    expert_in,
    gate_w,
    up_w,
    down_w,
    enc_w,
    dec_w,
    tok_all,
    gu_own,
    gu_ring,
    gu_in,
    gu_zsend,
    gu_zin,
    pre_f32,
    pre_send,
    pre_ring,
    pre_in,
    z_send,
    z_in,
    z_own,
    act,
    hid,
    out_send,
    out_in,
    rec,
    mate_in,
    fin_send,
    fin_in,
    fin_own,
    combine,
    row_own,
    row_mate,
    row_part,
    row_in,
    row_sum,
    row_zin,
    rows_dec,
    load_sem,
    sent,
    tz_r,
    ty_r,
    mate_r,
    gux_r,
    guz_r,
    hz_r,
    hx_r,
    px_r,
    pz_r,
    az_r,
    ax_r,
    out_r,
    cm_r,
    fin_r,
    rm_r,
    ry_r,
    rz_r,
    rg_r,
):
    e = lax.axis_index("exp")
    f = lax.axis_index("feat")
    chip, core = e // 2, e % 2
    y, zl = chip // 4, chip % 4
    zh, x = f // 4, f % 4
    mate = {"exp": chip * 2 + (1 - core), "feat": f}
    zpeer = {"exp": e, "feat": (1 - zh) * 4 + x}

    def xpeer(k):
        return {"exp": e, "feat": zh * 4 + (x + k) % 4}

    load_enc = pltpu.make_async_copy(enc_hbm, enc_w, load_sem.at[0])
    load_gate = pltpu.make_async_copy(gate_hbm.at[0], gate_w, load_sem.at[1])
    load_up = pltpu.make_async_copy(up_hbm.at[0], up_w, load_sem.at[2])
    load_dec = pltpu.make_async_copy(dec_hbm, dec_w.at[:, pl.ds(0, WIDTH)], load_sem.at[3])
    load_down = pltpu.make_async_copy(down_hbm.at[0], down_w, load_sem.at[4])
    small = [
        pltpu.make_async_copy(source, target, load_sem.at[5 + n])
        for n, (source, target) in enumerate(
            (
                (route_hbm, route_ref),
                (weight_hbm, weight_ref),
                (tok_hbm, tok_all.at[e, :, pl.ds(0, WIDTH)]),
                (ids_hbm, ids_ref),
                (values_hbm, values_ref),
                (bias_hbm, bias_ref),
            )
        )
    ]
    for load in small:
        load.start()
    for load in (load_enc, load_gate, load_up, load_dec, load_down):
        load.start()

    barrier = pltpu.get_barrier_semaphore()

    def greet(k, carry):
        pl.semaphore_signal(
            barrier, inc=1, device_id={"exp": (e + k) % EXPERTS, "feat": f}, device_id_type=MESH
        )
        return carry

    lax.fori_loop(1, EXPERTS, greet, 0)
    for k in (1, 3):
        pl.semaphore_signal(barrier, inc=1, device_id=xpeer(k), device_id_type=MESH)
    pl.semaphore_signal(barrier, inc=1, device_id=zpeer, device_id_type=MESH)
    small[0].wait()
    small[1].wait()
    expert_of = lax.broadcasted_iota(jnp.int32, (EXTRA, ROWS), 0)
    named = jnp.zeros((EXTRA, ROWS), F32)
    spread = jnp.zeros((EXTRA, ROWS), F32)
    for k in range(route_ref.shape[0]):
        hit = route_ref[k : k + 1, :] == expert_of
        named = jnp.where(hit, 1.0, named)
        spread = jnp.where(hit, weight_ref[k : k + 1, :], spread)
    one = lax.broadcasted_iota(jnp.int32, (ROWS, ROWS), 0)
    other = lax.broadcasted_iota(jnp.int32, (ROWS, ROWS), 1)
    before = dot(named.astype(BF16), jnp.where(one < other, 1.0, 0.0).astype(BF16))
    code_t = jnp.where((named > 0) & (before < SLOT), before + 1.0, 0.0).astype(BF16)
    code = lax.dot_general(
        jnp.where(one == other, 1.0, 0.0).astype(BF16),
        code_t,
        (((1,), (1,)), ((), ())),
        preferred_element_type=F32,
    ).astype(BF16)
    small[2].wait()
    tok_all[e, :, pl.ds(WIDTH, EXTRA)] = code
    pl.semaphore_wait(barrier, EXPERTS - 1 + 3)

    def same_core(there_y, there_z):
        return {"exp": (there_y * 4 + there_z) * 2 + core, "feat": f}

    def block_at(back_y, back_z, which):
        return (((y + 4 - back_y) % 4) * 4 + (zl + 4 - back_z) % 4) * 2 + which

    def token_z(k):
        return remote(
            tok_all.at[e], tok_all.at[e], sent.at[0], tz_r.at[k - 1], same_core(y, (zl + k) % 4)
        )

    def token_z_arrival(k):
        block = block_at(0, k, core)
        return remote(tok_all.at[block], tok_all.at[block], sent.at[0], tz_r.at[k - 1], mate)

    def token_y(k, m):
        block = block_at(0, m, core)
        at = (k - 1) * 4 + m
        return remote(
            tok_all.at[block], tok_all.at[block], sent.at[0], ty_r.at[at], same_core((y + k) % 4, zl)
        )

    def token_y_arrival(k, m):
        block = block_at(k, m, core)
        at = (k - 1) * 4 + m
        return remote(tok_all.at[block], tok_all.at[block], sent.at[0], ty_r.at[at], mate)

    def token_pass(k, m):
        block = block_at(k, m, core)
        return remote(tok_all.at[block], tok_all.at[block], sent.at[0], mate_r.at[k], mate)

    def four_passed(k):
        four = tok_all.at[pl.ds(0, 4)]
        return remote(four, four, sent.at[0], mate_r.at[k], mate)

    for k in (1, 3, 2):
        token_z(k).start()
    token_pass(0, 0).start()
    for k in (2, 1, 3):
        token_y(k, 0).start()
    for m in (1, 3, 2):
        token_z_arrival(m).wait_recv()
        token_pass(0, m).start()
        for k in (2, 1, 3):
            token_y(k, m).start()

    def from_y(k):
        for m in (0, 1, 3, 2):
            token_y_arrival(k, m).wait_recv()
            token_pass(k, m).start()

    def from_mate(k):
        four_passed(k).wait_recv()

    clamps = ids_ref.shape[1]

    def three(value):
        high = value.astype(BF16)
        rest = value - high.astype(F32)
        middle = rest.astype(BF16)
        return high, middle, (rest - middle.astype(F32)).astype(BF16)

    def route_weights():
        slot_lane = lax.broadcasted_iota(jnp.int32, (EXTRA, EXPERTS * SLOT), 1)
        widen = jnp.where(
            (slot_lane >> 3) == lax.broadcasted_iota(jnp.int32, (EXTRA, EXPERTS * SLOT), 0), 1.0, 0.0
        ).astype(BF16)
        slot_wanted = (
            (lax.broadcasted_iota(jnp.int32, (ROWS, EXPERTS * SLOT), 1) & 7) + 1
        ).astype(F32)
        in_slot = dot(code, widen) == slot_wanted

        for part, piece in enumerate(three(spread)):
            widened = lax.dot_general(
                piece, widen, (((0,), (0,)), ((), ())), preferred_element_type=F32
            )
            combine[part] = jnp.where(in_slot, widened, 0.0).astype(BF16)

    def listed_columns():
        small[3].wait()
        feature = lax.broadcasted_iota(jnp.int32, (FEATURES, clamps), 0) + e * FEATURES
        listed_col = jnp.where(feature == ids_ref[...], 1.0, 0.0).astype(BF16)
        dec_w[:, pl.ds(WIDTH, EXTRA)] = jnp.concatenate(
            [listed_col, jnp.zeros((FEATURES, EXTRA - clamps), BF16)], axis=1
        )

    toward = (1, 3)

    def quarter(k):
        return (x + k) % 4

    def half_rows(k, half, size):
        return pl.ds(pl.multiple_of(quarter(k) * 2 * size + half * size, size), size)

    def gu_rows(h, k, half):
        return pl.ds(pl.multiple_of(h * 128 + quarter(k) * 32 + half * 16, 16), 16)

    def gu_ring_copy(h, n):
        return remote(
            gu_own.at[gu_rows(h, 2, n)],
            gu_ring.at[h, n],
            sent.at[1],
            gux_r.at[h, n],
            xpeer(toward[n]),
        )

    def gu_early(h, n):
        return remote(
            gu_own.at[gu_rows(h, toward[n], 1 - n)],
            gu_in.at[h, 1 - n, 0],
            sent.at[1],
            gux_r.at[h, 2],
            xpeer(toward[n]),
        )

    def gu_late(h, n):
        return remote(
            gu_own.at[gu_rows(h, toward[n], n)],
            gu_in.at[h, n, 1],
            sent.at[1],
            gux_r.at[h, 2],
            xpeer(toward[n]),
        )

    def gu_relay(h):
        for n in (0, 1):
            gu_ring_copy(h, n).wait_recv()
            rows = gu_rows(h, toward[n], n)
            gu_own[rows, :] = gu_own[rows, :] + gu_ring[h, n]
            gu_late(h, n).start()

    def gu_pick():
        everything = tok_all[...].reshape(EXPERTS * ROWS, WIDE)
        pick = jnp.where(lax.broadcasted_iota(jnp.int32, (8, EXTRA), 1) == e, 1.0, 0.0).astype(BF16)
        codes = lax.dot_general(
            pick, everything[:, WIDTH:], (((1,), (1,)), ((), ())), preferred_element_type=F32
        )
        slot_row = lax.broadcasted_iota(jnp.int32, (EXPERTS * SLOT, EXPERTS * ROWS), 0)
        token_col = lax.broadcasted_iota(jnp.int32, (EXPERTS * SLOT, EXPERTS * ROWS), 1)
        same_block = (((slot_row >> 3) + e) & (EXPERTS - 1)) == (token_col >> 4)
        wanted = ((slot_row & 7) + 1).astype(F32)
        picker = jnp.where(same_block & (codes[0:1, :] == wanted), 1.0, 0.0).astype(BF16)
        expert_in[...] = dot(picker, everything[:, :WIDTH]).astype(BF16)
        load_gate.wait()
        load_up.wait()

    def gu_multiply(h):
        rows = pl.ds(h * 128, 128)
        for half, weights in ((0, gate_w), (1, up_w)):

            def gate_tile(n, carry, half=half, weights=weights):
                at = pl.multiple_of(n * 256, 256)
                gu_own[rows, pl.ds(pl.multiple_of(half * HIDDEN + n * 256, 256), 256)] = dot(
                    expert_in[rows, :], weights[:, pl.ds(at, 256)]
                )
                return carry

            lax.fori_loop(0, HIDDEN // 256, gate_tile, 0)
        for n in (0, 1):
            gu_ring_copy(h, n).start()
        for n in (0, 1):
            gu_early(h, n).start()

    def blocks_of(j):
        return ((y + j) % 4) * 8

    def pre_ring_copy(j, n):
        return remote(
            pre_send.at[j, half_rows(2, n, 16)],
            pre_ring.at[j, n],
            sent.at[2],
            px_r.at[j, n],
            xpeer(toward[n]),
        )

    def pre_early(j, n):
        return remote(
            pre_send.at[j, half_rows(toward[n], 1 - n, 16)],
            pre_in.at[j, 1 - n, 0],
            sent.at[2],
            px_r.at[j, 2],
            xpeer(toward[n]),
        )

    def pre_late(j, n):
        return remote(
            pre_send.at[j, half_rows(toward[n], n, 16)],
            pre_in.at[j, n, 1],
            sent.at[2],
            px_r.at[j, 2],
            xpeer(toward[n]),
        )

    def pre_relay(j):
        for n in (0, 1):
            pre_ring_copy(j, n).wait_recv()
            rows = half_rows(toward[n], n, 16)
            pre_send[j, rows, :] = (pre_f32[j, rows, :] + pre_ring[j, n].astype(F32)).astype(BF16)
            pre_late(j, n).start()

    def pre_multiply(j):
        rows = tok_all[pl.ds(blocks_of(j), 8)].reshape(CHUNK_ROWS, WIDE)[:, :WIDTH]

        def tile(n, carry):
            at = pl.multiple_of(n * 256, 256)
            part = dot(rows, enc_w[:, pl.ds(at, 256)])
            pre_f32[j, :, pl.ds(at, 256)] = part
            pre_send[j, :, pl.ds(at, 256)] = part.astype(BF16)
            return carry

        lax.fori_loop(0, FEATURES // 256, tile, 0)
        for n in (0, 1):
            pre_ring_copy(j, n).start()
        for n in (0, 1):
            pre_early(j, n).start()

    def pz_copy(j):
        return remote(z_send.at[j], z_in.at[j], sent.at[2], pz_r.at[j], zpeer)

    def pre_reduce(j):
        remote(pre_in.at[j], pre_in.at[j], sent.at[2], px_r.at[j, 2], mate).wait_recv()
        for keep in (0, 1):
            half = 1 - zh if keep == 0 else zh
            total = pre_f32[j, half_rows(0, half, 16), :]
            for k in range(2):
                total = total + pre_in[j, half, k].astype(F32)
            if keep == 0:
                z_send[j] = total.astype(BF16)
                pz_copy(j).start()
            else:
                z_own[j] = total

    def owned(j):
        return blocks_of(j) + 2 * x + zh

    def passed(j):
        return blocks_of(j) + 2 * x + (1 - zh)

    def az_copy(j):
        return remote(act.at[owned(j)], act.at[owned(j)], sent.at[3], az_r.at[j], zpeer)

    def block_of(j, k, side):
        return blocks_of(j) + 2 * quarter(k) + side

    def ax_copy(j, n, second):
        block = passed(j) if second else owned(j)
        at = n if n == second else 2
        return remote(act.at[block], act.at[block], sent.at[3], ax_r.at[j, at], xpeer(toward[n]))

    def ax_relay(j, n):
        block = block_of(j, toward[1 - n], zh if n == 0 else 1 - zh)
        return remote(
            act.at[block], act.at[block], sent.at[3], ax_r.at[j, 2], xpeer(toward[n])
        )

    def activate(j):
        pz_copy(j).wait_recv()
        if j == 0:
            small[5].wait()
        pre = z_own[j] + z_in[j].astype(F32) + bias_ref[...]
        act[owned(j)] = jnp.maximum(pre, 0.0).astype(BF16)
        az_copy(j).start()
        for n in (0, 1):
            ax_copy(j, n, 0).start()

    def pass_on(j):
        az_copy(j).wait_recv()
        for n in (1, 0):
            ax_copy(j, n, 1).start()

    def relay(j):
        ax_copy(j, 0, 0).wait_recv()
        ax_relay(j, 0).start()
        ax_copy(j, 1, 1).wait_recv()
        ax_relay(j, 1).start()

    def guz_copy(h):
        return remote(gu_zsend.at[h], gu_zin.at[h], sent.at[1], guz_r.at[h], zpeer)

    def gu_reduce(h):
        remote(gu_in.at[h], gu_in.at[h], sent.at[1], gux_r.at[h, 2], mate).wait_recv()
        for keep in (0, 1):
            half = 1 - zh if keep == 0 else zh
            mine = gu_rows(h, 0, half)
            total = gu_own[mine, :] + gu_in[h, half, 0] + gu_in[h, half, 1]
            if keep == 0:
                gu_zsend[h] = total
                guz_copy(h).start()
            else:
                gu_own[mine, :] = total

    def hid_of(h, k, side):
        return h * 8 + 2 * quarter(k) + side

    def hz_copy(h):
        part = hid_of(h, 0, zh)
        return remote(hid.at[part], hid.at[part], sent.at[4], hz_r.at[h], zpeer)

    def hx_copy(h, n, second):
        part = hid_of(h, 0, (1 - zh) if second else zh)
        at = n if n == second else 2
        return remote(hid.at[part], hid.at[part], sent.at[4], hx_r.at[h, at], xpeer(toward[n]))

    def hx_relay(h, n):
        part = hid_of(h, toward[1 - n], zh if n == 0 else 1 - zh)
        return remote(hid.at[part], hid.at[part], sent.at[4], hx_r.at[h, 2], xpeer(toward[n]))

    def gu_activate(h):
        guz_copy(h).wait_recv()
        total = gu_own[gu_rows(h, 0, zh), :] + gu_zin[h]
        gate, up = total[:, :HIDDEN], total[:, HIDDEN:]
        hid[hid_of(h, 0, zh)] = (gate / (1.0 + jnp.exp(-gate)) * up).astype(BF16)
        hz_copy(h).start()
        for n in (0, 1):
            hx_copy(h, n, 0).start()

    def gu_pass_on(h):
        hz_copy(h).wait_recv()
        for n in (1, 0):
            hx_copy(h, n, 1).start()

    def hid_relay(h):
        hx_copy(h, 0, 0).wait_recv()
        hx_relay(h, 0).start()
        hx_copy(h, 1, 1).wait_recv()
        hx_relay(h, 1).start()

    def out_copy(k):
        there = (e + k) % EXPERTS
        return remote(
            out_send.at[k], out_in.at[e], sent.at[5], out_r.at[0], {"exp": there, "feat": f}
        )

    def down(h):
        four = hid.at[pl.ds(0, 4)]
        remote(four, four, sent.at[4], hx_r.at[h, 2], mate).wait_recv()
        if h == 0:
            load_down.wait()
        hidden = hid[pl.ds(h * 8, 8)].reshape(128, HIDDEN)
        for n in range(7):
            cols = pl.ds(n * 128, 128)
            out_send[pl.ds(h * 16, 16), :, cols] = (
                dot(hidden, down_w[:, cols]).reshape(16, SLOT, 128).astype(BF16)
            )
        if h == 0:
            out_in[e] = out_send[0]

        def start(k, carry):
            out_copy(k).start()
            return carry

        lax.fori_loop(1 if h == 0 else 16, h * 16 + 16, start, 0)

    def cm_copy(j):
        return remote(rec.at[j, 1 - core], mate_in.at[j], sent.at[6], cm_r.at[j], mate)

    def decode(j):
        four = act.at[pl.ds(0, 4)]
        remote(four, four, sent.at[3], ax_r.at[j, 2], mate).wait_recv()
        rows = act[pl.ds(blocks_of(j), 8)].reshape(CHUNK_ROWS, FEATURES)

        def tile(n, carry):
            at = pl.multiple_of(n * 256, 256)
            part = dot(rows, dec_w[:, pl.ds(at, 256)]).reshape(4, 2, ROWS, 256)
            for c in (0, 1):
                rec[j, c, :, :, pl.ds(at, 256)] = part[:, c]
            return carry

        lax.fori_loop(0, WIDE // 256, tile, 0)
        cm_copy(j).start()

    def fin_copy(j, k):
        there = ((y + j) % 4) * 4 + (zl + k) % 4
        at = j * 4 + k
        return remote(
            fin_send.at[j, k],
            fin_in.at[at],
            sent.at[7],
            fin_r.at[0],
            {"exp": there * 2 + core, "feat": f},
        )

    def finish(j):
        cm_copy(j).wait_recv()
        for k in range(4):
            to = (zl + k) % 4
            total = rec[j, core, to] + mate_in[j, to]
            if j == 0 and k == 0:
                fin_own[...] = total
            else:
                fin_send[j, k] = total.astype(BF16)
                fin_copy(j, k).start()

    def row_mate_copy():
        return remote(row_own, row_mate, sent.at[8], rm_r.at[0], mate)

    def row_y_copy(k):
        there = (y + k) % 4
        return remote(
            row_part.at[there], row_in.at[k - 1], sent.at[8], ry_r.at[k - 1], same_core(there, zl)
        )

    def row_z_copy(k):
        return remote(
            row_sum, row_zin.at[k - 1], sent.at[8], rz_r.at[k - 1], same_core(y, (zl + k) % 4)
        )

    def row_gather_copy(k):
        return remote(
            rows_dec.at[y], rows_dec.at[y], sent.at[8], rg_r.at[k - 1], same_core((y + k) % 4, zl)
        )

    def rows_start():
        mine = lax.dot_general(
            dec_w[:, pl.ds(WIDTH, EXTRA)],
            dec_w[:, pl.ds(0, WIDTH)],
            (((0,), (0,)), ((), ())),
            preferred_element_type=F32,
        )
        row_own[...] = mine[:64].astype(BF16).reshape(4, ROWS, WIDTH)
        row_mate_copy().start()

    def rows_y():
        row_mate_copy().wait_recv()
        row_part[...] = (row_own[...].astype(F32) + row_mate[...].astype(F32)).astype(BF16)
        for k in range(1, 4):
            row_y_copy(k).start()

    def rows_z():
        total = row_part[y].astype(F32)
        for k in range(1, 4):
            row_y_copy(k).wait_recv()
            total = total + row_in[k - 1].astype(F32)
        row_sum[...] = total.astype(BF16)
        for k in range(1, 4):
            row_z_copy(k).start()

    def rows_gather():
        total = row_sum[...].astype(F32)
        for k in range(1, 4):
            row_z_copy(k).wait_recv()
            total = total + row_zin[k - 1].astype(F32)
        rows_dec[y] = total.astype(BF16)
        for k in range(1, 4):
            row_gather_copy(k).start()

    def combine_moe():
        most = out_in.at[pl.ds(1, EXPERTS - 1)]
        remote(most, most, sent.at[5], out_r.at[0], mate).wait_recv()
        for n in range(7):
            cols = pl.ds(n * 128, 128)
            rows = out_in[:, :, cols].astype(F32).reshape(EXPERTS * SLOT, 128).astype(BF16)
            moe_ref[:, cols] = dot(combine[2], rows) + dot(combine[1], rows) + dot(combine[0], rows)
        write_moe.start()

    def total_up():
        most = fin_in.at[pl.ds(1, CHIPS - 1)]
        remote(most, most, sent.at[7], fin_r.at[0], mate).wait_recv()
        total = fin_own[...]
        for at in range(1, CHIPS):
            total = total + fin_in[at].astype(F32)
        recon_ref[...] = total[:, :WIDTH]
        write_recon.start()
        for k in range(1, 4):
            row_gather_copy(k).wait_recv()
        small[4].wait()
        change = values_ref[...].astype(F32) - total[:, WIDTH : WIDTH + clamps]
        listed = rows_dec[...].reshape(64, WIDTH)
        high, middle, low = three(change)
        shift_ref[...] = dot(low, listed) + dot(middle, listed) + dot(high, listed)
        write_shift.start()

    write_recon = pltpu.make_async_copy(recon_ref, recon_hbm, load_sem.at[11])
    write_moe = pltpu.make_async_copy(moe_ref, moe_hbm, load_sem.at[12])
    write_shift = pltpu.make_async_copy(shift_ref, shift_hbm, load_sem.at[13])

    from_mate(0)
    load_enc.wait()
    pre_multiply(0)
    for k in (1, 3, 2):
        from_y(k)
    for k in (1, 3, 2):
        from_mate(k)
    pre_relay(0)
    pre_multiply(1)
    pre_multiply(2)
    pre_reduce(0)
    gu_pick()
    gu_multiply(0)
    pre_relay(1)
    route_weights()
    pre_multiply(3)
    load_dec.wait()
    listed_columns()
    rows_start()
    activate(0)
    pre_relay(2)
    gu_multiply(1)
    pre_reduce(1)
    rows_y()
    pre_relay(3)
    pre_reduce(2)
    rows_z()
    gu_relay(0)
    pass_on(0)
    rows_gather()
    activate(1)
    pre_reduce(3)
    gu_relay(1)
    activate(2)
    gu_reduce(0)
    relay(0)
    pass_on(1)
    activate(3)
    pass_on(2)
    gu_reduce(1)
    gu_activate(0)
    decode(0)
    pass_on(3)
    relay(1)
    relay(2)
    finish(0)
    gu_pass_on(0)
    relay(3)
    decode(1)
    gu_activate(1)
    finish(1)
    hid_relay(0)
    decode(2)
    gu_pass_on(1)
    finish(2)
    down(0)
    decode(3)
    hid_relay(1)
    finish(3)
    down(1)
    total_up()
    combine_moe()

    for kind, ref in (
        (0, tok_all.at[pl.ds(0, 31)]),
        (1, gu_own.at[pl.ds(0, 224)]),
        (2, act.at[pl.ds(0, 28)]),
        (3, act.at[pl.ds(0, 28)]),
        (4, hid.at[pl.ds(0, 14)]),
        (5, out_send.at[pl.ds(1, 31)]),
        (6, mate_in),
        (7, fin_in.at[pl.ds(1, 15)]),
        (8, out_send.at[pl.ds(0, 26)]),
    ):
        remote(ref, ref, sent.at[kind], rm_r.at[0], mate).wait_send()
    for write in (write_recon, write_moe, write_shift):
        write.wait()


def fused(*operands):
    hbm = pl.BlockSpec(memory_space=pl.ANY)
    dma = pltpu.SemaphoreType.DMA
    scratch = [
        pltpu.VMEM((8, ROWS), jnp.int32),
        pltpu.VMEM((8, ROWS), F32),
        pltpu.VMEM((1, FEATURES), F32),
        pltpu.VMEM(operands[4].shape, jnp.int32),
        pltpu.VMEM(operands[5].shape, BF16),
        pltpu.VMEM((ROWS, WIDTH), F32),
        pltpu.VMEM((ROWS, WIDTH), F32),
        pltpu.VMEM((ROWS, WIDTH), F32),
        pltpu.VMEM((EXPERTS * SLOT, WIDTH), BF16),
        pltpu.VMEM((WIDTH, HIDDEN), BF16),
        pltpu.VMEM((WIDTH, HIDDEN), BF16),
        pltpu.VMEM((HIDDEN, WIDTH), BF16),
        pltpu.VMEM((WIDTH, FEATURES), BF16),
        pltpu.VMEM((FEATURES, WIDE), BF16),
        pltpu.VMEM((EXPERTS, ROWS, WIDE), BF16),
        pltpu.VMEM((EXPERTS * SLOT, 2 * HIDDEN), F32),
        pltpu.VMEM((2, 2, ROWS, 2 * HIDDEN), F32),
        pltpu.VMEM((2, 2, 2, ROWS, 2 * HIDDEN), F32),
        pltpu.VMEM((2, ROWS, 2 * HIDDEN), F32),
        pltpu.VMEM((2, ROWS, 2 * HIDDEN), F32),
        pltpu.VMEM((CHUNKS, CHUNK_ROWS, FEATURES), F32),
        pltpu.VMEM((CHUNKS, CHUNK_ROWS, FEATURES), BF16),
        pltpu.VMEM((CHUNKS, 2, ROWS, FEATURES), BF16),
        pltpu.VMEM((CHUNKS, 2, 2, ROWS, FEATURES), BF16),
        pltpu.VMEM((CHUNKS, ROWS, FEATURES), BF16),
        pltpu.VMEM((CHUNKS, ROWS, FEATURES), BF16),
        pltpu.VMEM((CHUNKS, ROWS, FEATURES), F32),
        pltpu.VMEM((EXPERTS, ROWS, FEATURES), BF16),
        pltpu.VMEM((2 * 8, ROWS, HIDDEN), BF16),
        pltpu.VMEM((EXPERTS, SLOT, WIDTH), BF16),
        pltpu.VMEM((EXPERTS, SLOT, WIDTH), BF16),
        pltpu.VMEM((CHUNKS, 2, 4, ROWS, WIDE), F32),
        pltpu.VMEM((CHUNKS, 4, ROWS, WIDE), F32),
        pltpu.VMEM((CHUNKS, 4, ROWS, WIDE), BF16),
        pltpu.VMEM((CHIPS, ROWS, WIDE), BF16),
        pltpu.VMEM((ROWS, WIDE), F32),
        pltpu.VMEM((3, ROWS, EXPERTS * SLOT), BF16),
        pltpu.VMEM((4, ROWS, WIDTH), BF16),
        pltpu.VMEM((4, ROWS, WIDTH), BF16),
        pltpu.VMEM((4, ROWS, WIDTH), BF16),
        pltpu.VMEM((3, ROWS, WIDTH), BF16),
        pltpu.VMEM((ROWS, WIDTH), BF16),
        pltpu.VMEM((3, ROWS, WIDTH), BF16),
        pltpu.VMEM((4, ROWS, WIDTH), BF16),
        dma((14,)),
        dma((9,)),
        dma((3,)),
        dma((12,)),
        dma((4,)),
        dma((2, 3)),
        dma((2,)),
        dma((2,)),
        dma((2, 3)),
        dma((CHUNKS, 3)),
        dma((CHUNKS,)),
        dma((CHUNKS,)),
        dma((CHUNKS, 3)),
        dma((1,)),
        dma((CHUNKS,)),
        dma((1,)),
        dma((1,)),
        dma((3,)),
        dma((3,)),
        dma((3,)),
    ]
    return pl.pallas_call(
        kernel,
        out_shape=(
            jax.ShapeDtypeStruct((ROWS, WIDTH), F32),
            jax.ShapeDtypeStruct((ROWS, WIDTH), F32),
            jax.ShapeDtypeStruct((ROWS, WIDTH), F32),
        ),
        in_specs=[hbm] * 11,
        out_specs=(hbm, hbm, hbm),
        scratch_shapes=scratch,
        name="fused_layer",
        cost_estimate=pl.CostEstimate(
            flops=6_000_000_000, bytes_accessed=400_000_000, transcendentals=0
        ),
        compiler_params=pltpu.CompilerParams(
            collective_id=0, has_side_effects=True, vmem_limit_bytes=56 << 20
        ),
    )(*operands)


def local(
    tokens,
    route_ids,
    route_weights,
    gate_proj,
    up_proj,
    down_proj,
    enc_weight,
    enc_bias,
    dec_weight,
    dec_bias,
    clamp_ids,
    clamp_values,
):
    recon, moe_out, shift = fused(
        tokens,
        route_ids.T,
        route_weights.T,
        enc_bias[None, :],
        clamp_ids[None, :],
        clamp_values[None, :],
        gate_proj,
        up_proj,
        down_proj,
        enc_weight,
        dec_weight,
    )
    return moe_out - recon - dec_bias, moe_out + shift


def solution(mesh):
    placed = (
        P("exp", "feat"),
        P("exp", None),
        P("exp", None),
        P("exp", "feat", None),
        P("exp", "feat", None),
        P("exp", None, "feat"),
        P("feat", "exp"),
        P("exp"),
        P("exp", "feat"),
        P("feat"),
        P(),
        P(),
    )
    return jax.shard_map(
        local,
        mesh=mesh,
        in_specs=placed,
        out_specs=(P("exp", "feat"), P("exp", "feat")),
        check_vma=False,
    )
```

time: 132 us -> 109 us (0.83)
  Pallas kernels: 129 us -> 106 us
    pallas_call x1, Pallas kernels: 129 us -> 106 us  [fused(): pl.pallas_call(kernel, out_shape=(jax.ShapeDtypeStruct((ROWS, WIDTH), F32...]
where the time goes in v3:
time: 109 us; the launch traced here: 108 us
  Pallas kernels  106 us (97%)
  other arithmetic  1.53 us (1%)
    pallas_call x1, Pallas kernels, fused(): pl.pallas_call(kernel, out_shape=(jax.ShapeDtypeStruct((ROWS, WIDTH), F32...  106 us

profile of v3, /device:TPU:1, one launch (start us, length us, event | category | flops | bytes accessed | tf_op | source)
XLA Modules:
  0.0 108.4 jit_solution(10475092844610255876)
XLA Ops:
  0.6 0.0 copy-start
  0.6 106.2 %fused_layer.1 = (f32[16,896]{1,0:T(8,128)}, f32[16,896]{1,0:T(8,128)}, f32[16,896]{1,0:T(8,128)}) custom-call(bf16[16,896]{1,0:T(8,128)(2,1)} %tok_hbm.1, s32[8,16]{1,0:T(8,128)} %bitcast.6, f32[8,16]{1,0:T(8,128)} %bitcast.7, f32[1,2048]{1,0:T(1,128)} %bitcast.5, s32[1,64]{1,0:T(1,128)} %bitcast.8, bf16[1,64]{1,0:T(2,128)(2,1)} %bitcast.9, ...), custom_call_target="tpu_custom_call" | custom-call | flops 6000000000 | bytes 400000000 | tf_op jit(solution)/shard_map/fused_layer/pallas_call | solution.py:814
  106.9 0.0 copy-done
  106.9 1.5 %fusion = (f32[16,896]{1,0:T(8,128)}, f32[16,896]{1,0:T(8,128)}) fusion(f32[16,896]{1,0:T(8,128)} %get-tuple-element.5, f32[16,896]{1,0:T(8,128)} %get-tuple-element.7, f32[896]{0:T(1024)S(1)} %copy-done, f32[16,896]{1,0:T(8,128)} %get-tuple-element.6), kind=kLoop, calls=%fused_computation.1 | loop fusion | flops 43008 | bytes 290304 | tf_op jit(solution)/shard_map/add | solution.py:861
Async XLA Ops:
  0.6 106.3 %copy-start = (f32[896]{0:T(1024)S(1)}, f32[896]{0:T(1024)}, u32[]{:S(2)}) copy-start(f32[896]{0:T(1024)} %param.21) | copy-start | bytes 10756

commit v4 on v3

--- a/solution.py
+++ b/solution.py
@@ -89,6 +89,8 @@
     fin_send,
     fin_in,
     fin_own,
+    fin_zsend,
+    fin_zin,
     combine,
     row_own,
     row_mate,
@@ -108,7 +110,6 @@
     hx_r,
     px_r,
     pz_r,
-    az_r,
     ax_r,
     out_r,
     cm_r,
@@ -408,54 +409,34 @@
 
     def pre_reduce(j):
         remote(pre_in.at[j], pre_in.at[j], sent.at[2], px_r.at[j, 2], mate).wait_recv()
-        for keep in (0, 1):
-            half = 1 - zh if keep == 0 else zh
+        for half in (0, 1):
             total = pre_f32[j, half_rows(0, half, 16), :]
             for k in range(2):
                 total = total + pre_in[j, half, k].astype(F32)
-            if keep == 0:
-                z_send[j] = total.astype(BF16)
-                pz_copy(j).start()
-            else:
-                z_own[j] = total
-
-    def owned(j):
-        return blocks_of(j) + 2 * x + zh
-
-    def passed(j):
-        return blocks_of(j) + 2 * x + (1 - zh)
-
-    def az_copy(j):
-        return remote(act.at[owned(j)], act.at[owned(j)], sent.at[3], az_r.at[j], zpeer)
+            z_own[j, half] = total
+            z_send[j, half] = total.astype(BF16)
+        pz_copy(j).start()
 
     def block_of(j, k, side):
         return blocks_of(j) + 2 * quarter(k) + side
 
-    def ax_copy(j, n, second):
-        block = passed(j) if second else owned(j)
-        at = n if n == second else 2
+    def ax_copy(j, n, side):
+        block = block_of(j, 0, side)
+        at = n if n == side else 2
         return remote(act.at[block], act.at[block], sent.at[3], ax_r.at[j, at], xpeer(toward[n]))
 
     def ax_relay(j, n):
-        block = block_of(j, toward[1 - n], zh if n == 0 else 1 - zh)
-        return remote(
-            act.at[block], act.at[block], sent.at[3], ax_r.at[j, 2], xpeer(toward[n])
-        )
+        block = block_of(j, toward[1 - n], n)
+        return remote(act.at[block], act.at[block], sent.at[3], ax_r.at[j, 2], xpeer(toward[n]))
 
     def activate(j):
         pz_copy(j).wait_recv()
-        if j == 0:
-            small[5].wait()
-        pre = z_own[j] + z_in[j].astype(F32) + bias_ref[...]
-        act[owned(j)] = jnp.maximum(pre, 0.0).astype(BF16)
-        az_copy(j).start()
-        for n in (0, 1):
-            ax_copy(j, n, 0).start()
-
-    def pass_on(j):
-        az_copy(j).wait_recv()
-        for n in (1, 0):
-            ax_copy(j, n, 1).start()
+        for side in (0, 1):
+            pre = z_own[j, side] + z_in[j, side].astype(F32) + bias_ref[...]
+            act[block_of(j, 0, side)] = jnp.maximum(pre, 0.0).astype(BF16)
+        for side in (0, 1):
+            for n in (0, 1):
+                ax_copy(j, n, n if side == 0 else 1 - n).start()
 
     def relay(j):
         ax_copy(j, 0, 0).wait_recv()
@@ -473,7 +454,7 @@
             mine = gu_rows(h, 0, half)
             total = gu_own[mine, :] + gu_in[h, half, 0] + gu_in[h, half, 1]
             if keep == 0:
-                gu_zsend[h] = total
+                gu_zsend[h] = total.astype(BF16)
                 guz_copy(h).start()
             else:
                 gu_own[mine, :] = total
@@ -496,7 +477,7 @@
 
     def gu_activate(h):
         guz_copy(h).wait_recv()
-        total = gu_own[gu_rows(h, 0, zh), :] + gu_zin[h]
+        total = gu_own[gu_rows(h, 0, zh), :] + gu_zin[h].astype(F32)
         gate, up = total[:, :HIDDEN], total[:, HIDDEN:]
         hid[hid_of(h, 0, zh)] = (gate / (1.0 + jnp.exp(-gate)) * up).astype(BF16)
         hz_copy(h).start()
@@ -523,8 +504,6 @@
     def down(h):
         four = hid.at[pl.ds(0, 4)]
         remote(four, four, sent.at[4], hx_r.at[h, 2], mate).wait_recv()
-        if h == 0:
-            load_down.wait()
         hidden = hid[pl.ds(h * 8, 8)].reshape(128, HIDDEN)
         for n in range(7):
             cols = pl.ds(n * 128, 128)
@@ -558,27 +537,40 @@
         lax.fori_loop(0, WIDE // 256, tile, 0)
         cm_copy(j).start()
 
-    def fin_copy(j, k):
-        there = ((y + j) % 4) * 4 + (zl + k) % 4
-        at = j * 4 + k
-        return remote(
-            fin_send.at[j, k],
-            fin_in.at[at],
-            sent.at[7],
-            fin_r.at[0],
-            {"exp": there * 2 + core, "feat": f},
+    def fin_copy(j):
+        return remote(
+            fin_send.at[j], fin_in.at[j], sent.at[7], fin_r.at[0], same_core((y + j) % 4, zl)
+        )
+
+    def fin_z_copy(k):
+        return remote(
+            fin_zsend.at[k], fin_zin.at[k], sent.at[7], fin_r.at[1], same_core(y, (zl + k) % 4)
         )
 
     def finish(j):
         cm_copy(j).wait_recv()
-        for k in range(4):
+        for to in range(4):
+            total = rec[j, core, to] + mate_in[j, to]
+            if j == 0:
+                fin_own[to] = total
+            else:
+                fin_send[j, to] = total.astype(BF16)
+        if j > 0:
+            fin_copy(j).start()
+
+    def finish_z():
+        most = fin_in.at[pl.ds(1, 3)]
+        remote(most, most, sent.at[7], fin_r.at[0], mate).wait_recv()
+        for k in (1, 3, 2, 0):
             to = (zl + k) % 4
-            total = rec[j, core, to] + mate_in[j, to]
-            if j == 0 and k == 0:
-                fin_own[...] = total
+            total = fin_own[to]
+            for j in range(1, CHUNKS):
+                total = total + fin_in[j, to].astype(F32)
+            if k == 0:
+                fin_zin[0] = total
             else:
-                fin_send[j, k] = total.astype(BF16)
-                fin_copy(j, k).start()
+                fin_zsend[k] = total
+                fin_z_copy(k).start()
 
     def row_mate_copy():
         return remote(row_own, row_mate, sent.at[8], rm_r.at[0], mate)
@@ -643,11 +635,9 @@
         write_moe.start()
 
     def total_up():
-        most = fin_in.at[pl.ds(1, CHIPS - 1)]
-        remote(most, most, sent.at[7], fin_r.at[0], mate).wait_recv()
-        total = fin_own[...]
-        for at in range(1, CHIPS):
-            total = total + fin_in[at].astype(F32)
+        most = fin_zin.at[pl.ds(1, 3)]
+        remote(most, most, sent.at[7], fin_r.at[1], mate).wait_recv()
+        total = (fin_zin[0] + fin_zin[1]) + (fin_zin[2] + fin_zin[3])
         recon_ref[...] = total[:, :WIDTH]
         write_recon.start()
         for k in range(1, 4):
@@ -670,71 +660,70 @@
         from_y(k)
     for k in (1, 3, 2):
         from_mate(k)
+    gu_pick()
     pre_relay(0)
-    pre_multiply(1)
     pre_multiply(2)
+    gu_multiply(1)
+    pre_multiply(3)
+    pre_relay(2)
+    gu_multiply(0)
     pre_reduce(0)
-    gu_pick()
-    gu_multiply(0)
-    pre_relay(1)
-    route_weights()
-    pre_multiply(3)
     load_dec.wait()
     listed_columns()
     rows_start()
-    activate(0)
-    pre_relay(2)
-    gu_multiply(1)
-    pre_reduce(1)
+    gu_relay(1)
+    pre_multiply(1)
+    pre_relay(3)
     rows_y()
-    pre_relay(3)
+    route_weights()
     pre_reduce(2)
     rows_z()
     gu_relay(0)
-    pass_on(0)
+    small[5].wait()
+    activate(0)
+    gu_reduce(1)
+    pre_relay(1)
+    activate(2)
     rows_gather()
+    pre_reduce(3)
+    gu_reduce(0)
+    gu_activate(1)
+    relay(0)
+    pre_reduce(1)
+    relay(2)
+    activate(3)
+    decode(0)
+    decode(2)
+    finish(0)
+    relay(3)
+    gu_pass_on(1)
+    gu_activate(0)
+    finish(2)
     activate(1)
-    pre_reduce(3)
-    gu_relay(1)
-    activate(2)
-    gu_reduce(0)
-    relay(0)
-    pass_on(1)
-    activate(3)
-    pass_on(2)
-    gu_reduce(1)
-    gu_activate(0)
-    decode(0)
-    pass_on(3)
-    relay(1)
-    relay(2)
-    finish(0)
-    gu_pass_on(0)
-    relay(3)
-    decode(1)
-    gu_activate(1)
-    finish(1)
-    hid_relay(0)
-    decode(2)
-    gu_pass_on(1)
-    finish(2)
-    down(0)
     decode(3)
     hid_relay(1)
+    gu_pass_on(0)
+    relay(1)
     finish(3)
+    load_down.wait()
     down(1)
+    hid_relay(0)
+    decode(1)
+    down(0)
+    finish(1)
+    finish_z()
+    combine_moe()
     total_up()
-    combine_moe()
 
     for kind, ref in (
         (0, tok_all.at[pl.ds(0, 31)]),
-        (1, gu_own.at[pl.ds(0, 224)]),
-        (2, act.at[pl.ds(0, 28)]),
-        (3, act.at[pl.ds(0, 28)]),
+        (1, gu_own.at[pl.ds(0, 208)]),
+        (2, act),
+        (3, act.at[pl.ds(0, 24)]),
         (4, hid.at[pl.ds(0, 14)]),
         (5, out_send.at[pl.ds(1, 31)]),
         (6, mate_in),
-        (7, fin_in.at[pl.ds(1, 15)]),
+        (7, tok_all.at[pl.ds(0, 18)]),
         (8, out_send.at[pl.ds(0, 26)]),
     ):
         remote(ref, ref, sent.at[kind], rm_r.at[0], mate).wait_send()
@@ -764,15 +753,15 @@
         pltpu.VMEM((EXPERTS * SLOT, 2 * HIDDEN), F32),
         pltpu.VMEM((2, 2, ROWS, 2 * HIDDEN), F32),
         pltpu.VMEM((2, 2, 2, ROWS, 2 * HIDDEN), F32),
-        pltpu.VMEM((2, ROWS, 2 * HIDDEN), F32),
-        pltpu.VMEM((2, ROWS, 2 * HIDDEN), F32),
+        pltpu.VMEM((2, ROWS, 2 * HIDDEN), BF16),
+        pltpu.VMEM((2, ROWS, 2 * HIDDEN), BF16),
         pltpu.VMEM((CHUNKS, CHUNK_ROWS, FEATURES), F32),
         pltpu.VMEM((CHUNKS, CHUNK_ROWS, FEATURES), BF16),
         pltpu.VMEM((CHUNKS, 2, ROWS, FEATURES), BF16),
         pltpu.VMEM((CHUNKS, 2, 2, ROWS, FEATURES), BF16),
-        pltpu.VMEM((CHUNKS, ROWS, FEATURES), BF16),
-        pltpu.VMEM((CHUNKS, ROWS, FEATURES), BF16),
-        pltpu.VMEM((CHUNKS, ROWS, FEATURES), F32),
+        pltpu.VMEM((CHUNKS, 2, ROWS, FEATURES), BF16),
+        pltpu.VMEM((CHUNKS, 2, ROWS, FEATURES), BF16),
+        pltpu.VMEM((CHUNKS, 2, ROWS, FEATURES), F32),
         pltpu.VMEM((EXPERTS, ROWS, FEATURES), BF16),
         pltpu.VMEM((2 * 8, ROWS, HIDDEN), BF16),
         pltpu.VMEM((EXPERTS, SLOT, WIDTH), BF16),
@@ -780,8 +769,10 @@
         pltpu.VMEM((CHUNKS, 2, 4, ROWS, WIDE), F32),
         pltpu.VMEM((CHUNKS, 4, ROWS, WIDE), F32),
         pltpu.VMEM((CHUNKS, 4, ROWS, WIDE), BF16),
-        pltpu.VMEM((CHIPS, ROWS, WIDE), BF16),
-        pltpu.VMEM((ROWS, WIDE), F32),
+        pltpu.VMEM((CHUNKS, 4, ROWS, WIDE), BF16),
+        pltpu.VMEM((4, ROWS, WIDE), F32),
+        pltpu.VMEM((4, ROWS, WIDE), F32),
+        pltpu.VMEM((4, ROWS, WIDE), F32),
         pltpu.VMEM((3, ROWS, EXPERTS * SLOT), BF16),
         pltpu.VMEM((4, ROWS, WIDTH), BF16),
         pltpu.VMEM((4, ROWS, WIDTH), BF16),
@@ -801,11 +792,10 @@
         dma((2, 3)),
         dma((CHUNKS, 3)),
         dma((CHUNKS,)),
-        dma((CHUNKS,)),
         dma((CHUNKS, 3)),
         dma((1,)),
         dma((CHUNKS,)),
-        dma((1,)),
+        dma((2,)),
         dma((1,)),
         dma((3,)),
         dma((3,)),

time: 109 us -> 98.8 us (0.906)
  Pallas kernels: 106 us -> 96.4 us
    pallas_call x1, Pallas kernels: 106 us -> 96.4 us  [fused(): pl.pallas_call(kernel, out_shape=(jax.ShapeDtypeStruct((ROWS, WIDTH), F32...]
where the time goes in v4:
time: 98.8 us; the launch traced here: 98.6 us
  Pallas kernels  96.4 us (98%)
  other arithmetic  1.53 us (2%)
    pallas_call x1, Pallas kernels, fused(): pl.pallas_call(kernel, out_shape=(jax.ShapeDtypeStruct((ROWS, WIDTH), F32...  96.4 us

profile of v4, /device:TPU:1, one launch (start us, length us, event | category | flops | bytes accessed | tf_op | source)
XLA Modules:
  0.0 98.6 jit_solution(3602544586465119135)
XLA Ops:
  0.6 0.0 copy-start
  0.6 96.4 %fused_layer.1 = (f32[16,896]{1,0:T(8,128)}, f32[16,896]{1,0:T(8,128)}, f32[16,896]{1,0:T(8,128)}) custom-call(bf16[16,896]{1,0:T(8,128)(2,1)} %tok_hbm.1, s32[8,16]{1,0:T(8,128)} %bitcast.6, f32[8,16]{1,0:T(8,128)} %bitcast.7, f32[1,2048]{1,0:T(1,128)} %bitcast.5, s32[1,64]{1,0:T(1,128)} %bitcast.8, bf16[1,64]{1,0:T(2,128)(2,1)} %bitcast.9, ...), custom_call_target="tpu_custom_call" | custom-call | flops 6000000000 | bytes 400000000 | tf_op jit(solution)/shard_map/fused_layer/pallas_call | solution.py:804
  97.0 0.0 copy-done
  97.0 1.5 %fusion = (f32[16,896]{1,0:T(8,128)}, f32[16,896]{1,0:T(8,128)}) fusion(f32[16,896]{1,0:T(8,128)} %get-tuple-element.5, f32[16,896]{1,0:T(8,128)} %get-tuple-element.7, f32[896]{0:T(1024)S(1)} %copy-done, f32[16,896]{1,0:T(8,128)} %get-tuple-element.6), kind=kLoop, calls=%fused_computation.1 | loop fusion | flops 43008 | bytes 290304 | tf_op jit(solution)/shard_map/add | solution.py:851
Async XLA Ops:
  0.6 96.4 %copy-start = (f32[896]{0:T(1024)S(1)}, f32[896]{0:T(1024)}, u32[]{:S(2)}) copy-start(f32[896]{0:T(1024)} %param.21) | copy-start | bytes 10756

commit v5 on v4

--- a/solution.py
+++ b/solution.py
@@ -662,55 +662,55 @@
         from_mate(k)
     gu_pick()
     pre_relay(0)
+    pre_multiply(1)
+    gu_multiply(1)
     pre_multiply(2)
-    gu_multiply(1)
-    pre_multiply(3)
-    pre_relay(2)
+    pre_reduce(0)
+    pre_relay(1)
     gu_multiply(0)
-    pre_reduce(0)
     load_dec.wait()
     listed_columns()
     rows_start()
     gu_relay(1)
-    pre_multiply(1)
-    pre_relay(3)
+    pre_multiply(3)
     rows_y()
     route_weights()
-    pre_reduce(2)
+    pre_relay(2)
     rows_z()
-    gu_relay(0)
     small[5].wait()
     activate(0)
+    pre_reduce(1)
+    gu_relay(0)
+    rows_gather()
     gu_reduce(1)
-    pre_relay(1)
+    pre_relay(3)
+    activate(1)
+    pre_reduce(2)
+    relay(0)
+    gu_activate(1)
+    gu_reduce(0)
+    pre_reduce(3)
+    relay(1)
     activate(2)
-    rows_gather()
-    pre_reduce(3)
-    gu_reduce(0)
-    gu_activate(1)
-    relay(0)
-    pre_reduce(1)
+    decode(0)
+    gu_pass_on(1)
+    decode(1)
+    gu_activate(0)
     relay(2)
+    finish(0)
+    hid_relay(1)
+    finish(1)
     activate(3)
-    decode(0)
     decode(2)
-    finish(0)
-    relay(3)
-    gu_pass_on(1)
-    gu_activate(0)
-    finish(2)
-    activate(1)
-    decode(3)
-    hid_relay(1)
     gu_pass_on(0)
-    relay(1)
-    finish(3)
     load_down.wait()
     down(1)
+    relay(3)
+    finish(2)
     hid_relay(0)
-    decode(1)
+    decode(3)
     down(0)
-    finish(1)
+    finish(3)
     finish_z()
     combine_moe()
     total_up()

time: 98.8 us -> 97.3 us (0.985)
  Pallas kernels: 96.4 us -> 94.9 us
    pallas_call x1, Pallas kernels: 96.4 us -> 94.9 us  [fused(): pl.pallas_call(kernel, out_shape=(jax.ShapeDtypeStruct((ROWS, WIDTH), F32...]
where the time goes in v5:
time: 97.3 us; the launch traced here: 97.1 us
  Pallas kernels  94.9 us (98%)
  other arithmetic  1.53 us (2%)
    pallas_call x1, Pallas kernels, fused(): pl.pallas_call(kernel, out_shape=(jax.ShapeDtypeStruct((ROWS, WIDTH), F32...  94.9 us

profile of v5, /device:TPU:1, one launch (start us, length us, event | category | flops | bytes accessed | tf_op | source)
XLA Modules:
  0.0 97.1 jit_solution(40604109578014130)
XLA Ops:
  0.6 0.0 copy-start
  0.6 94.9 %fused_layer.1 = (f32[16,896]{1,0:T(8,128)}, f32[16,896]{1,0:T(8,128)}, f32[16,896]{1,0:T(8,128)}) custom-call(bf16[16,896]{1,0:T(8,128)(2,1)} %tok_hbm.1, s32[8,16]{1,0:T(8,128)} %bitcast.6, f32[8,16]{1,0:T(8,128)} %bitcast.7, f32[1,2048]{1,0:T(1,128)} %bitcast.5, s32[1,64]{1,0:T(1,128)} %bitcast.8, bf16[1,64]{1,0:T(2,128)(2,1)} %bitcast.9, ...), custom_call_target="tpu_custom_call" | custom-call | flops 6000000000 | bytes 400000000 | tf_op jit(solution)/shard_map/fused_layer/pallas_call | solution.py:804
  95.6 0.0 copy-done
  95.6 1.5 %fusion = (f32[16,896]{1,0:T(8,128)}, f32[16,896]{1,0:T(8,128)}) fusion(f32[16,896]{1,0:T(8,128)} %get-tuple-element.5, f32[16,896]{1,0:T(8,128)} %get-tuple-element.7, f32[896]{0:T(1024)S(1)} %copy-done, f32[16,896]{1,0:T(8,128)} %get-tuple-element.6), kind=kLoop, calls=%fused_computation.1 | loop fusion | flops 43008 | bytes 290304 | tf_op jit(solution)/shard_map/add | solution.py:851
Async XLA Ops:
  0.6 95.0 %copy-start = (f32[896]{0:T(1024)S(1)}, f32[896]{0:T(1024)}, u32[]{:S(2)}) copy-start(f32[896]{0:T(1024)} %param.21) | copy-start | bytes 10756
